TPU v7x, 32 devices: a whole 2x2x4 slice. The times are simulated.
32 devices in a mesh: parts: 2 (over x), elec: 4 (over y, core), walk: 4 (over z).
Axes of the slice: x: 2, y: 2, z: 4, core: 2. Of those that a mesh axis runs over, the one named last changes fastest.
Arguments:
- elec_pos: float32 [3, 32, 512], P(None, ('parts', 'walk'), 'elec'), parts along dimension 1, may hold values from -8 to 8
- atom_pos: float32 [200, 3], P(('parts', 'elec')), parts along dimension 0, may hold values from -8 to 8
- atom_emb: float32 [200, 256], P(('parts', 'elec')), parts along dimension 0, may hold values from -6 to 6
- spin_emb: float32 [2, 256], replicated, may hold values from -6 to 6
- spin: int32 [1024], P(('parts', 'elec')), parts along dimension 0, may hold values from 0 to 1, as said below
- near_atoms: int32 [16, 2], P('parts'), parts along dimension 0, may hold values from 0 to 3
- pair_list: int32 [16, 4], P('parts'), parts along dimension 0, may hold values from 0 to 7, as said below
- pair_count: int32 [16], P('parts'), parts along dimension 0, may hold values from 1 to 4, as said below
- w_query: bfloat16 [256, 256], replicated, may hold values from -64 to 64
- w_key: bfloat16 [256, 256], replicated, may hold values from -0.375 to 0.375
- w_value: bfloat16 [256, 256], replicated, may hold values from -0.375 to 0.375
- w_out: bfloat16 [256, 256], replicated, may hold values from -0.375 to 0.375
- w_orb: bfloat16 [2, 256, 1024], replicated, may hold values from -0.375 to 0.375
- target: bfloat16 [32, 512, 1024], P(('parts', 'walk'), 'elec'), parts along dimension 0, may hold values from -6 to 6
Outputs:
- grad_orb: float32 [4, 256, 1024], P('parts'), parts along dimension 0
- grad_out: float32 [512, 256], P('parts'), parts along dimension 0
- loss: float32 [2], P('parts'), parts along dimension 0
There are 2 independent parts, one for each index of `parts`. A program takes and returns all parts, laid end to end along the dimension named above; an argument that names none is the same for every part. Nothing has to cross between parts.
Inputs may be any that keep to these rules, and one draw needn't show every extreme that they name: `pair_list`: row b lists 4 distinct blocks, the first being b itself; every listed c has c // 2 equal to b // 2 or one more or one less than it, modulo 8 / 2. Only the first pair_count[b] entries of row b are listed; some block lists all 4. Each aligned run of 128 electrons holds exactly half of each spin.
All inputs are finite; a program needn't handle non-finite values.
Results may differ from a plain program's by a relative error of at most 0.002.
Values may be sent and summed in bfloat16 or wider, within the bound.
A program may use at most 64 MiB of HBM per device.

v0:
```python
import math

import jax
import jax.numpy as jnp
from jax import lax
from jax.sharding import PartitionSpec as P

HEADS = 16
BLOCK = 64
ATOM_DEV = 25
NEAR = 2
KMAX = 4


def shifted(block, axis, distance):
    devices = range(lax.axis_size(axis))
    route = [((i - distance) % len(devices), i) for i in devices]
    return lax.ppermute(block, axis, route)


def local(
    elec_pos,
    atom_pos,
    atom_emb,
    spin_emb,
    spin,
    near_atoms,
    pair_list,
    pair_count,
    w_query,
    w_key,
    w_value,
    w_out,
    w_orb,
    target,
):
    walkers = elec_pos.shape[1]
    local_rows = elec_pos.shape[2]
    per_device = local_rows // BLOCK
    elec_count = lax.axis_size("elec")
    elec_index = lax.axis_index("elec")
    model_width = w_query.shape[0]
    head_size = model_width // HEADS
    orbital_count = w_orb.shape[2]
    row_local = walkers * local_rows
    half_rows = local_rows // 2
    all_pos, all_emb = (
        lax.all_gather(atom_pos, "elec", axis=0, tiled=True),
        lax.all_gather(atom_emb, "elec", axis=0, tiled=True),
    )
    my_blocks = elec_index * per_device + jnp.arange(per_device)
    near_here = jnp.take(near_atoms, my_blocks, axis=0)
    near_pos = jnp.take(all_pos.reshape(elec_count, ATOM_DEV, 3), near_here, axis=0).reshape(
        per_device, NEAR * ATOM_DEV, 3
    )
    near_emb = jnp.take(
        all_emb.reshape(elec_count, ATOM_DEV, model_width), near_here, axis=0
    ).reshape(per_device, NEAR * ATOM_DEV, model_width)
    positions = elec_pos.reshape(3, walkers, per_device, BLOCK)
    distance = jnp.zeros((walkers, per_device, BLOCK, NEAR * ATOM_DEV), jnp.float32)
    for axis_id in range(3):
        spacing = positions[axis_id][..., None] - near_pos[None, :, None, :, axis_id]
        distance = distance + spacing * spacing
    closeness = 1.0 / (1.0 + distance)
    atom_term = jnp.einsum(
        "wbea,bad->wbed", closeness, near_emb, precision=lax.Precision.HIGHEST
    ).reshape(walkers, local_rows, model_width)
    spin_rows = jnp.where(spin[:, None] == 1, spin_emb[1][None, :], spin_emb[0][None, :])
    hidden = (atom_term + spin_rows[None]).astype(jnp.bfloat16)
    flat_rows = hidden.reshape(row_local, model_width)
    queries = (
        jnp.dot(flat_rows, w_query, preferred_element_type=jnp.float32)
        .astype(jnp.bfloat16)
        .reshape(walkers, local_rows, HEADS, head_size)
    )
    key_rows = (
        jnp.dot(flat_rows, w_key, preferred_element_type=jnp.float32)
        .astype(jnp.bfloat16)
        .reshape(walkers, local_rows, model_width)
    )
    value_rows = (
        jnp.dot(flat_rows, w_value, preferred_element_type=jnp.float32)
        .astype(jnp.bfloat16)
        .reshape(walkers, local_rows, model_width)
    )
    block_count = elec_count * per_device
    lists_here = jnp.take(pair_list, my_blocks, axis=0)
    counts_here = jnp.take(pair_count, my_blocks, axis=0)
    slot_ids = jnp.arange(KMAX)
    in_list = slot_ids[None, :] < counts_here[:, None]
    listed = jnp.any(
        (lists_here[:, :, None] == jnp.arange(block_count)[None, None, :]) & in_list[:, :, None],
        axis=1,
    )
    score_scale = 1.0 / math.sqrt(head_size)

    def attend_piece(running, key_part, value_part, key_blocks):
        old_max, old_total, old_acc = running
        key_count = key_part.shape[1]
        allowed = jnp.repeat(jnp.take(listed, key_blocks, axis=1), BLOCK, axis=0)
        key_mask = allowed[None, :, None, :]
        key_heads = key_part.reshape(walkers, key_count, HEADS, head_size)
        value_heads = value_part.reshape(walkers, key_count, HEADS, head_size)
        scores = (
            jnp.einsum("wqhd,wkhd->wqhk", queries, key_heads, preferred_element_type=jnp.float32)
            * score_scale
        )
        scores = jnp.where(key_mask, scores, -1e30)
        new_max = jnp.maximum(old_max, jnp.max(scores, axis=3))
        weights = jnp.where(key_mask, jnp.exp(scores - new_max[..., None]), 0.0)
        factor = jnp.exp(old_max - new_max)
        new_total = old_total * factor + jnp.sum(weights, axis=3)
        new_acc = old_acc * factor[..., None] + jnp.einsum(
            "wqhk,wkhd->wqhd",
            weights.astype(jnp.bfloat16),
            value_heads,
            preferred_element_type=jnp.float32,
        )
        return (new_max, new_total, new_acc)

    def shard_blocks(owner):
        return (owner * local_rows + jnp.arange(local_rows)) // BLOCK

    lower_owner = (elec_index + elec_count - 1) % elec_count
    upper_owner = (elec_index + 1) % elec_count
    initial = (
        jnp.full((walkers, local_rows, HEADS), -1e30, jnp.float32),
        jnp.zeros((walkers, local_rows, HEADS), jnp.float32),
        jnp.zeros((walkers, local_rows, HEADS, head_size), jnp.float32),
    )
    lower_kv = shifted((key_rows, value_rows), "elec", 1)
    upper_kv = shifted((key_rows, value_rows), "elec", -1)
    running = attend_piece(initial, key_rows, value_rows, shard_blocks(elec_index))
    running = attend_piece(running, lower_kv[0], lower_kv[1], shard_blocks(lower_owner))
    running = attend_piece(running, upper_kv[0], upper_kv[1], shard_blocks(upper_owner))
    final_max, final_total, final_acc = running
    attended = (
        (final_acc / final_total[..., None]).astype(jnp.bfloat16).reshape(row_local, model_width)
    )
    mixed_out = jnp.dot(attended, w_out, preferred_element_type=jnp.float32)
    hidden_out = (flat_rows.astype(jnp.float32) + mixed_out).astype(jnp.bfloat16)
    by_spin = jnp.argsort(spin, stable=True)
    sorted_hidden = jnp.take(hidden_out.reshape(walkers, local_rows, model_width), by_spin, axis=1)
    sorted_attended = jnp.take(attended.reshape(walkers, local_rows, model_width), by_spin, axis=1)
    sorted_target = jnp.take(target, by_spin, axis=1)
    loss_part = jnp.float32(0.0)
    orb_terms = []
    out_part = jnp.zeros((model_width, model_width), jnp.float32)
    for spin_id in range(2):
        hidden_group = sorted_hidden[:, spin_id * half_rows : (spin_id + 1) * half_rows].reshape(
            walkers * half_rows, model_width
        )
        attended_group = sorted_attended[
            :, spin_id * half_rows : (spin_id + 1) * half_rows
        ].reshape(walkers * half_rows, model_width)
        target_group = sorted_target[:, spin_id * half_rows : (spin_id + 1) * half_rows].reshape(
            walkers * half_rows, orbital_count
        )
        orbitals = jnp.dot(hidden_group, w_orb[spin_id], preferred_element_type=jnp.float32)
        residual = orbitals - target_group.astype(jnp.float32)
        loss_part = loss_part + 0.5 * jnp.sum(residual * residual)
        signal = residual.astype(jnp.bfloat16)
        orb_terms.append(
            lax.dot_general(
                hidden_group, signal, (((0,), (0,)), ((), ())), preferred_element_type=jnp.float32
            )
        )
        backward = lax.dot_general(
            signal, w_orb[spin_id], (((1,), (1,)), ((), ())), preferred_element_type=jnp.float32
        ).astype(jnp.bfloat16)
        out_part = out_part + lax.dot_general(
            attended_group, backward, (((0,), (0,)), ((), ())), preferred_element_type=jnp.float32
        )
    orb_part = jnp.stack(orb_terms, axis=0)
    orb_sum, out_sum, loss_sum = lax.psum((orb_part, out_part, loss_part), ("elec", "walk"))
    rows_float = jnp.float32(row_local * elec_count * lax.axis_size("walk"))
    grad_orb = orb_sum / rows_float
    grad_out = out_sum / rows_float
    loss = jnp.reshape(loss_sum / rows_float, (1,))
    return (grad_orb, grad_out, loss)


def solution(mesh):
    in_specs = (
        P(None, ("parts", "walk"), "elec"),
        P(("parts", "elec"), None),
        P(("parts", "elec"), None),
        P(),
        P(("parts", "elec")),
        P("parts", None),
        P("parts", None),
        P("parts"),
        P(),
        P(),
        P(),
        P(),
        P(),
        P(("parts", "walk"), "elec", None),
    )
    out_specs = (P("parts", None, None), P("parts", None), P("parts"))
    return jax.shard_map(local, mesh=mesh, in_specs=in_specs, out_specs=out_specs, check_vma=False)
```

profile of v0, /device:TPU:0, one launch (start us, length us, event | category | flops | bytes accessed | tf_op | source)
XLA Modules:
  0.0 197.2 jit_solution(5505594694340146671)
XLA Ops:
  9.0 6.3 %all-gather.1 = f32[4,25,3]{1,2,0:T(4,128)S(1)} all-gather(f32[1,25,3]{1,2,0:T(4,128)} %bitcast.217), channel_id=1, replica_groups=mesh['parts'=2,'elec'=4,'walk'=4] {'elec'}, dimensions={0}, use_global_device_ids=true | all-gather | bytes 1500 | tf_op jit(solution)/shard_map/all_gather | solution.py:48
  16.1 5.8 %all-gather = f32[4,25,256]{2,1,0:T(8,128)S(1)} all-gather(f32[1,25,256]{2,1,0:T(8,128)} %bitcast.214), channel_id=1, replica_groups=mesh['parts'=2,'elec'=4,'walk'=4] {'elec'}, dimensions={0}, use_global_device_ids=true | all-gather | bytes 128000 | tf_op jit(solution)/shard_map/all_gather | solution.py:49
  26.6 1.4 collective-permute-start.2
  29.3 2.5 %sort.17 = (s32[128]{0:T(128)}, s32[128]{0:T(128)S(1)}) sort(s32[128]{0:T(128)S(1)} %copy-done.14, s32[128]{0:T(128)S(1)} %iota.37), dimensions={0}, to_apply=%region_7.9 | sort | flops 896 | bytes 2048 | tf_op jit(solution)/shard_map/jit(argsort)/sort | solution.py:142
  37.9 3.7 %gather_fusion.5 = bf16[128,4,1024]{2,0,1:T(8,128)(2,1)S(1)} fusion(bf16[4,128,1024]{2,1,0:T(8,128)(2,1)S(1)} %copy-done, s32[1024]{0:T(1024)S(1)} %pad_clamp_fusion), kind=kCustom, calls=%fused_computation.10 | custom fusion | bytes 2097664 | tf_op jit(solution)/shard_map/jit(_take)/gather | solution.py:145
  41.7 2.9 %fusion = (f32[4,128,16]{1,2,0:T(8,128)S(1)}, f32[4,16,128,128]{3,2,1,0:T(8,128)}) fusion(pred[128,128]{0,1:T(8,128)(4,1)S(1)} %copy.146, bf16[4,128,16,16]{1,0,3,2:T(4,128)(2,1)S(1)} %reshape.316, bf16[4,128,16,16]{1,0,3,2:T(4,128)(2,1)S(1)} %reshape_reshape.9), kind=kOutput, calls=%fused_computation.17 | convolution fusion | flops 36691968 | bytes 4767744 | tf_op jit(solution)/shard_map/wqhd,wkhd->wqhk/dot_general | solution.py:105
  44.6 1.1 fusion.117
  46.9 2.8 %fusion.1 = (f32[4,128,16]{1,2,0:T(8,128)S(1)}, f32[4,16,128,128]{3,2,1,0:T(8,128)}) fusion(pred[128,128]{0,1:T(8,128)(4,1)S(1)} %copy.156, bf16[4,128,16,16]{1,3,2,0:T(8,128)(2,1)S(1)} %bitcast.193, bf16[4,128,16,16]{1,0,3,2:T(4,128)(2,1)S(1)} %reshape.316), kind=kOutput, calls=%fused_computation.18 | convolution fusion | flops 36691968 | bytes 4767744 | tf_op jit(solution)/shard_map/wqhd,wkhd->wqhk/dot_general | solution.py:105
  49.7 1.1 copy.164
  51.8 1.3 fusion.7
  53.7 2.1 %copy-done.3 = f32[4,16,128,128]{3,2,1,0:T(8,128)S(1)} copy-done((f32[4,16,128,128]{3,2,1,0:T(8,128)S(1)}, f32[4,16,128,128]{3,2,1,0:T(8,128)}, u32[]{:S(2)}) %copy-start.3) | copy-done | bytes 4194328
  55.8 2.3 %fusion.3 = (f32[4,128,16]{1,2,0:T(8,128)S(1)}, f32[4,128,16]{1,2,0:T(8,128)S(1)}) fusion(f32[4,16,128,128]{3,2,1,0:T(8,128)S(1)} %copy-done.3, f32[4,128,16]{1,2,0:T(8,128)S(1)} %get-tuple-element.21, pred[128,128]{0,1:T(8,128)(4,1)S(1)} %copy.146, f32[4,128,16]{1,2,0:T(8,128)S(1)} %get-tuple-element.13, f32[4,16,128,128]{3,2,1,0:T(8,128)S(1)} %copy-done.2, ...), kind=kLoop, calls=%fused_computation.20 | loop fusion | flops 10469376 | bytes 8552448 | tf_op jit(solution)/shard_map/reduce_sum | solution.py:112
  58.2 1.8 fusion.33
  61.1 3.1 %fusion.24 = f32[4,128,16,16]{1,3,2,0:T(8,128)S(1)} fusion(bf16[4,128,16,16]{1,3,2,0:T(8,128)(2,1)S(1)} %bitcast.207, f32[4,16,128,128]{3,2,1,0:T(8,128)} %copy-done.4, f32[4,128,16]{1,2,0:T(8,128)S(1)} %get-tuple-element.12, pred[128,128]{0,1:T(8,128)(4,1)S(1)} %copy.163), kind=kOutput, calls=%fused_computation.39 | convolution fusion | flops 38797312 | bytes 5029888 | tf_op jit(solution)/shard_map/wqhk,wkhd->wqhd/dot_general | solution.py:113
  64.2 1.1 copy.159
  65.3 3.3 %fusion.47 = bf16[4,128,16,16]{1,3,2,0:T(8,128)(2,1)S(1)} fusion(f32[4,128,16,16]{1,3,2,0:T(8,128)S(1)} %fusion.24, f32[4,128,16,16]{1,3,2,0:T(8,128)} %fusion.33, bf16[4,128,16,16]{1,3,2,0:T(8,128)(2,1)S(1)} %bitcast.206, f32[4,16,128,128]{3,2,1,0:T(8,128)} %get-tuple-element.35, f32[4,128,16]{1,2,0:T(8,128)S(1)} %get-tuple-element.13, ...), kind=kOutput, calls=%fused_computation.60 | convolution fusion | flops 39452672 | bytes 5881856 | tf_op jit(solution)/shard_map/wqhk,wkhd->wqhd/dot_general | solution.py:113
  71.9 2.2 %multiply_reduce_fusion.1 = (f32[]{:T(128)}, bf16[256,1024]{1,0:T(8,128)(2,1)S(1)}) fusion(bf16[256,1024]{1,0:T(8,128)(2,1)} %bitcast.200, bf16[256,256]{1,0:T(8,128)(2,1)S(1)} %bitcast.203, bf16[2,256,1024]{2,1,0:T(8,128)(2,1)} %param.30), kind=kOutput, calls=%fused_computation.57 | convolution fusion | flops 135528448 | bytes 1703940 | tf_op jit(solution)/shard_map/dot_general | solution.py:159
  74.4 2.3 %fusion.43 = f32[256,256]{1,0:T(8,128)} fusion(bf16[256,256]{1,0:T(8,128)(2,1)S(1)} %bitcast.210, bf16[2,256,1024]{2,1,0:T(8,128)(2,1)} %param.30, bf16[256,1024]{1,0:T(8,128)(2,1)S(1)} %get-tuple-element.39), kind=kOutput, calls=%fused_computation.54 | convolution fusion | flops 167837696 | bytes 1441792 | tf_op jit(solution)/shard_map/dot_general | solution.py:171
  76.8 2.1 %multiply_reduce_fusion = (f32[]{:T(128)}, bf16[256,1024]{1,0:T(8,128)(2,1)S(1)}) fusion(bf16[256,1024]{1,0:T(8,128)(2,1)S(1)} %bitcast.199, bf16[256,256]{1,0:T(8,128)(2,1)S(1)} %bitcast.201, bf16[2,256,1024]{2,1,0:T(8,128)(2,1)} %param.30), kind=kOutput, calls=%fused_computation.56 | convolution fusion | flops 135528448 | bytes 1703940 | tf_op jit(solution)/shard_map/dot_general | solution.py:159
  80.0 2.5 %convolution_add_fusion.1 = f32[256,256]{1,0:T(8,128)} fusion(f32[256,256]{1,0:T(8,128)} %fusion.43, bf16[256,256]{1,0:T(8,128)(2,1)S(1)} %bitcast.205, bf16[2,256,1024]{2,1,0:T(8,128)(2,1)} %param.30, bf16[256,1024]{1,0:T(8,128)(2,1)} %copy-done.5), kind=kOutput, calls=%fused_computation.51 | convolution fusion | flops 167903232 | bytes 1703936 | tf_op jit(solution)/shard_map/dot_general | solution.py:171
  82.5 1.5 pad_maximum_fusion
  85.2 35.5 %psum.23 = f32[]{:T(128)} all-reduce(f32[]{:T(128)S(6)} %add.215), channel_id=1, replica_groups=mesh['parts'=2,'elec'=4,'walk'=4] {'elec','walk'}, use_global_device_ids=true, to_apply=%region_12.15 | all-reduce | flops 1 | bytes 8 | tf_op jit(solution)/shard_map/psum | solution.py:175
  121.4 63.9 %all-reduce.3.cloned.1.call-done = (f32[2,256,1024]{2,1,0:T(8,128)}, f32[256,256]{1,0:T(8,128)}) async-done(((f32[2,256,1024]{2,1,0:T(8,128)}, f32[256,256]{1,0:T(8,128)}), (f32[2,256,1024]{2,1,0:T(8,128)}, f32[256,256]{1,0:T(8,128)})) %all-reduce.3.cloned.1.call-update) | async-done | bytes 2359312 | tf_op jit(solution)/shard_map/psum | solution.py:175
  185.2 3.3 %broadcast_multiply_fusion = f32[2,256,1024]{2,1,0:T(8,128)} fusion(f32[2,256,1024]{2,1,0:T(8,128)} %get-tuple-element.7), kind=kLoop, calls=%fused_computation.58 | loop fusion | flops 524288 | bytes 4194304 | tf_op jit(solution)/shard_map/div | solution.py:177
  (136 shorter events, 23.5 us)
Async XLA Ops:
  7.2 30.7 %copy-start = (bf16[4,128,1024]{2,1,0:T(8,128)(2,1)S(1)}, bf16[4,128,1024]{2,1,0:T(8,128)(2,1)}, u32[]{:S(2)}) copy-start(bf16[4,128,1024]{2,1,0:T(8,128)(2,1)} %param.31) | copy-start | bytes 3145732
  7.2 22.1 %copy-start.14 = (s32[128]{0:T(128)S(1)}, s32[128]{0:T(128)}, u32[]{:S(2)}) copy-start(s32[128]{0:T(128)} %param.22) | copy-start | bytes 1540
  7.2 18.8 %copy-start.9 = (bf16[256,256]{1,0:T(8,128)(2,1)S(1)}, bf16[256,256]{1,0:T(8,128)(2,1)}, u32[]{:S(2)}) copy-start(bf16[256,256]{1,0:T(8,128)(2,1)} %param.27) | copy-start | bytes 393220
  7.2 20.8 %copy-start.10 = (bf16[256,256]{1,0:T(8,128)(2,1)S(1)}, bf16[256,256]{1,0:T(8,128)(2,1)}, u32[]{:S(2)}) copy-start(bf16[256,256]{1,0:T(8,128)(2,1)} %param.28) | copy-start | bytes 393220
  7.2 24.6 %copy-start.12 = (s32[8,4]{0,1:T(4,128)S(1)}, s32[8,4]{0,1:T(4,128)}, u32[]{:S(2)}) copy-start(s32[8,4]{0,1:T(4,128)} %param.24) | copy-start | bytes 388
  7.2 25.3 %copy-start.1 = (s32[8]{0:T(128)S(1)}, s32[8]{0:T(128)}, u32[]{:S(2)}) copy-start(s32[8]{0:T(128)} %param.25) | copy-start | bytes 100
  7.2 27.3 %copy-start.11 = (bf16[256,256]{1,0:T(8,128)(2,1)S(1)}, bf16[256,256]{1,0:T(8,128)(2,1)}, u32[]{:S(2)}) copy-start(bf16[256,256]{1,0:T(8,128)(2,1)} %param.26) | copy-start | bytes 393220
  7.2 178.0 %all-reduce.3.cloned.1.call-start = ((), (), s32[]{:S(2)}) async-start(), calls=%async_computation | async-start | bytes 4718592 | tf_op jit(solution)/shard_map/psum | solution.py:175
  26.2 19.6 %collective-permute-start = (bf16[4,128,256]{2,1,0:T(8,128)(2,1)S(1)}, bf16[4,128,256]{2,1,0:T(8,128)(2,1)}, u32[]{:S(2)}, u32[]{:S(2)}) collective-permute-start(bf16[4,128,256]{2,1,0:T(8,128)(2,1)S(1)} %bitcast.196), channel_id=1, source_target_pairs={{12,0},{0,4},{4,8},{8,12},{13,1},{1,5},{5,9},{9,13},{14,2},{2,6},{... | collective-permute-start | bytes 786440 | tf_op jit(solution)/shard_map/ppermute | solution.py:18
  26.6 23.1 %collective-permute-start.2 = (bf16[4,128,256]{2,1,0:T(8,128)(2,1)S(1)}, bf16[4,128,256]{2,1,0:T(8,128)(2,1)}, u32[]{:S(2)}, u32[]{:S(2)}) collective-permute-start(bf16[4,128,256]{2,1,0:T(8,128)(2,1)S(1)} %bitcast.197), channel_id=1, source_target_pairs={{4,0},{8,4},{12,8},{0,12},{5,1},{9,5},{13,9},{1,13},{6,2},{10,6},{... | collective-permute-start | bytes 786440 | tf_op jit(solution)/shard_map/ppermute | solution.py:18
  28.3 31.7 %collective-permute-start.3 = (bf16[4,128,256]{2,1,0:T(8,128)(2,1)S(1)}, bf16[4,128,256]{2,1,0:T(8,128)(2,1)}, u32[]{:S(2)}, u32[]{:S(2)}) collective-permute-start(bf16[4,128,256]{2,1,0:T(8,128)(2,1)S(1)} %bitcast.194), channel_id=1, source_target_pairs={{4,0},{8,4},{12,8},{0,12},{5,1},{9,5},{13,9},{1,13},{6,2},{10,6},{... | collective-permute-start | bytes 786440 | tf_op jit(solution)/shard_map/ppermute | solution.py:18
  28.7 35.4 %collective-permute-start.1 = (bf16[4,128,256]{2,1,0:T(8,128)(2,1)S(1)}, bf16[4,128,256]{2,1,0:T(8,128)(2,1)}, u32[]{:S(2)}, u32[]{:S(2)}) collective-permute-start(bf16[4,128,256]{2,1,0:T(8,128)(2,1)S(1)} %bitcast.195), channel_id=1, source_target_pairs={{12,0},{0,4},{4,8},{8,12},{13,1},{1,5},{5,9},{9,13},{14,2},{2,6},{... | collective-permute-start | bytes 786440 | tf_op jit(solution)/shard_map/ppermute | solution.py:18
  50.8 2.9 %copy-start.2 = (f32[4,16,128,128]{3,2,1,0:T(8,128)S(1)}, f32[4,16,128,128]{3,2,1,0:T(8,128)}, u32[]{:S(2)}) copy-start(f32[4,16,128,128]{3,2,1,0:T(8,128)} %get-tuple-element.35) | copy-start | bytes 12582916
  50.8 5.0 %copy-start.3 = (f32[4,16,128,128]{3,2,1,0:T(8,128)S(1)}, f32[4,16,128,128]{3,2,1,0:T(8,128)}, u32[]{:S(2)}) copy-start(f32[4,16,128,128]{3,2,1,0:T(8,128)} %get-tuple-element.37) | copy-start | bytes 12582916
  51.8 6.3 %copy-start.4 = (f32[4,16,128,128]{3,2,1,0:T(8,128)}, f32[4,16,128,128]{3,2,1,0:T(8,128)S(1)}, u32[]{:S(2)}) copy-start(f32[4,16,128,128]{3,2,1,0:T(8,128)S(1)} %get-tuple-element.33) | copy-start | bytes 12582916
  55.8 2.3 %copy-start.7 = (bf16[4,128,16,16]{1,0,3,2:T(4,128)(2,1)S(1)}, bf16[4,128,16,16]{1,0,3,2:T(4,128)(2,1)}, u32[]{:S(2)}) copy-start(bf16[4,128,16,16]{1,0,3,2:T(4,128)(2,1)} %reshape_reshape.10) | copy-start | bytes 786436
  65.3 3.6 %copy-start.13 = (bf16[256,256]{1,0:T(8,128)(2,1)S(1)}, bf16[256,256]{1,0:T(8,128)(2,1)}, u32[]{:S(2)}) copy-start(bf16[256,256]{1,0:T(8,128)(2,1)} %param.29) | copy-start | bytes 393220
  71.2 5.5 %copy-start.6 = (bf16[4,64,1024]{2,1,0:T(8,128)(2,1)S(1)}, bf16[4,64,1024]{2,1,0:T(8,128)(2,1)}, u32[]{:S(2)}) copy-start(bf16[4,64,1024]{2,1,0:T(8,128)(2,1)} %get-tuple-element.15) | copy-start | bytes 1572868
  78.8 0.8 copy-start.5
  185.2 3.3 %copy-start.8 = (f32[256,256]{1,0:T(8,128)S(1)}, f32[256,256]{1,0:T(8,128)}, u32[]{:S(2)}) copy-start(f32[256,256]{1,0:T(8,128)} %get-tuple-element.8) | copy-start | bytes 786436
Sparse Core Ops, SparseCore 0:
  84.1 101.0 all-reduce.2
where the time goes:
time: 198 us; the launch traced here: 197 us
  waiting for transfers between devices  63.9 us (32%)
  blocking collectives  47.7 us (24%)
  matrix products  26.4 us (13%)
  local copies, waits for them, and re-layouts  25.5 us (13%)
  between operations  17.6 us (9%)
  other arithmetic  13.7 us (7%)
  starting transfers between devices  2.44 us (1%)
    psum x1, waiting for transfers between devices, local(): lax.psum((orb_part, out_part, loss_part), ('elec', 'walk'))  63.9 us
    psum x1, blocking collectives, local(): lax.psum((orb_part, out_part, loss_part), ('elec', 'walk'))  35.5 us
    dot_general x3, matrix products, attend_piece(): jnp.einsum('wqhk,wkhd->wqhd', weights.astype(jnp.bfloat16), value_heads,...  8.22 us
    dot_general x3, matrix products, attend_piece(): jnp.einsum('wqhd,wkhd->wqhk', queries, key_heads, preferred_element_type=...  6.68 us
    all_gather x1, blocking collectives, local(): lax.all_gather(atom_pos, 'elec', axis=0, tiled=True)  6.28 us
    all_gather x1, blocking collectives, local(): lax.all_gather(atom_emb, 'elec', axis=0, tiled=True)  5.85 us
    dot_general x2, matrix products, local(): lax.dot_general(attended_group, backward, (((0,), (0,)), ((), ())), prefe...  4.87 us
    unnamed x32, local copies, waits for them, and re-layouts  4.51 us
  transfers between devices with their start and end apart: 5, of which 1 were waited for; matrix products, arithmetic and copies ran while one was open for 16% of the time, Pallas kernels for 0%

commit v1 on v0

v1 whole, which is shorter than its diff:
```python
import math

import jax
import jax.numpy as jnp
from jax import lax
from jax.experimental import pallas as pl
from jax.experimental.pallas import tpu as pltpu
from jax.sharding import PartitionSpec as P

HEADS = 16
BLOCK = 64
ATOM_DEV = 25
NEAR = 2
KMAX = 4
SLOT = 32
LANES = 256
CHUNKS = 4
F32 = jnp.float32
BF16 = jnp.bfloat16
VM = pltpu.VMEM
NT = (((1,), (1,)), ((), ()))


def gather_kernel(count, emb, pos, epos, spin, gemb, gpos, gep, gsp, send, recv):
    me = lax.axis_index("elec")
    barrier = pltpu.get_barrier_semaphore()
    for k in range(count - 1):
        pl.semaphore_signal(
            barrier,
            inc=1,
            device_id={"elec": lax.rem(me + 1 + k, count)},
            device_id_type=pl.DeviceIdType.MESH,
        )
    pl.semaphore_wait(barrier, count - 1)
    copies = []
    for k in range(count - 1):
        peer = lax.rem(me + 1 + k, count)
        for i, (src, dst) in enumerate(((emb, gemb), (pos, gpos), (epos, gep), (spin, gsp))):
            copy = pltpu.make_async_remote_copy(
                src_ref=src,
                dst_ref=dst.at[me],
                send_sem=send.at[k, i],
                recv_sem=recv.at[k, i],
                device_id={"elec": peer},
                device_id_type=pl.DeviceIdType.MESH,
            )
            copy.start()
            copies.append(copy)
    gemb[me] = emb[...]
    gpos[me] = pos[...]
    gep[me] = epos[...]
    gsp[me] = spin[...]
    for copy in copies:
        copy.wait()


def compute_kernel(
    count,
    near,
    pairs,
    pair_n,
    gemb,
    gpos,
    gep,
    gsp,
    spin_emb,
    w_query,
    w_key,
    w_value,
    w_out,
    w_orb,
    target,
    total_ref,
    pstack,
    estack,
    q_s,
    k_s,
    vt_s,
    h_s,
    bias_s,
    att_s,
):
    me = lax.axis_index("elec")
    walkers, rows = gep.shape[2], gep.shape[3]
    width = w_query.shape[0]
    head = width // HEADS
    per_device = rows // BLOCK
    owners = (me, lax.rem(me + count - 1, count), lax.rem(me + 1, count))
    wv_t = w_value[...].astype(F32).T.astype(BF16)
    pstack[...] = jnp.zeros_like(pstack)
    estack[...] = jnp.zeros_like(estack)
    depth = per_device * NEAR * SLOT
    row_id = lax.broadcasted_iota(jnp.int32, (depth, rows), 0)
    lane_id = lax.broadcasted_iota(jnp.int32, (depth, rows), 1)
    block_mask = (row_id // (NEAR * SLOT)) == (lane_id // BLOCK)
    for j, owner in enumerate(owners):
        for p in range(per_device):
            for n in range(NEAR):
                slot = p * NEAR + n
                group = near[owner * per_device + p, n]
                pstack[j, slot * SLOT : slot * SLOT + ATOM_DEV, 0:3] = gpos[group]
                estack[j, slot * SLOT : slot * SLOT + ATOM_DEV, :] = gemb[group]
        estack[j, ATOM_DEV : ATOM_DEV + 2, :] = spin_emb[...]
        up_row = gsp[owner].astype(F32)
        electron = gep[owner]
        pieces = []
        for w in range(walkers):
            distance = jnp.zeros((depth, rows), F32)
            for axis in range(3):
                spacing = electron[axis, w : w + 1, :] - pstack[j, :, axis : axis + 1]
                distance = distance + spacing * spacing
            close = jnp.where(block_mask, 1.0 / (1.0 + distance), 0.0)
            close = jnp.where(row_id == ATOM_DEV, 1.0 - up_row, close)
            close = jnp.where(row_id == ATOM_DEV + 1, up_row, close)
            pieces.append(close.T)
        close_all = jnp.concatenate(pieces, axis=0)
        hidden = jnp.dot(
            close_all,
            estack[j],
            precision=lax.Precision.HIGHEST,
            preferred_element_type=F32,
        ).astype(BF16)
        keys = jnp.dot(hidden, w_key[...], preferred_element_type=F32).astype(BF16)
        values_t = lax.dot_general(wv_t, hidden, NT, preferred_element_type=F32).astype(BF16)
        for w in range(walkers):
            k_s[w, j * rows : (j + 1) * rows, :] = keys[w * rows : (w + 1) * rows]
            vt_s[w, :, j * rows : (j + 1) * rows] = values_t[:, w * rows : (w + 1) * rows]
        if j == 0:
            h_s[...] = hidden
            queries = jnp.dot(hidden, w_query[...], preferred_element_type=F32).astype(BF16)
            queries = queries.astype(F32) * (1.0 / math.sqrt(head))
            for w in range(walkers):
                q_s[w] = queries[w * rows : (w + 1) * rows]
    half_lane = lax.broadcasted_iota(jnp.int32, (BLOCK, 2 * rows), 1)
    for j, owner in enumerate(owners):
        for kb in range(per_device):
            key_block = owner * per_device + kb
            value = jnp.zeros((BLOCK, 2 * rows), F32)
            for p in range(per_device):
                query_block = me * per_device + p
                listed = None
                for slot in range(KMAX):
                    hit = jnp.logical_and(
                        pairs[query_block, slot] == key_block, slot < pair_n[query_block, 0]
                    )
                    listed = hit if listed is None else jnp.logical_or(listed, hit)
                level = jnp.where(listed, 0.0, -1e30).astype(F32)
                value = jnp.where(half_lane % rows // BLOCK == p, level, value)
            start = j * rows + kb * BLOCK
            bias_s[start : start + BLOCK, :] = value
    head_lane = lax.broadcasted_iota(jnp.int32, (rows, width), 1) // head

    def walker(w, carry):
        query = q_s[w]
        key = k_s[w]
        for pair in range(HEADS // 2):
            both = jnp.concatenate(
                [
                    jnp.where(head_lane == 2 * pair, query, 0.0),
                    jnp.where(head_lane == 2 * pair + 1, query, 0.0),
                ],
                axis=0,
            ).astype(BF16)
            scores = lax.dot_general(key, both, NT, preferred_element_type=F32) + bias_s[...]
            top = jnp.max(scores, axis=0, keepdims=True)
            weights = jnp.exp(scores - top)
            total = jnp.sum(weights, axis=0, keepdims=True)
            mixed = jnp.dot(
                vt_s[w, 2 * pair * head : 2 * (pair + 1) * head, :],
                weights.astype(BF16),
                preferred_element_type=F32,
            )
            mixed = mixed / total
            att_s[w, 2 * pair * head : (2 * pair + 1) * head, :] = mixed[:head, :rows]
            att_s[w, (2 * pair + 1) * head : 2 * (pair + 1) * head, :] = mixed[head:, rows:]
        return carry

    lax.fori_loop(0, walkers, walker, 0)
    att_t = jnp.concatenate([att_s[w].astype(BF16) for w in range(walkers)], axis=1)
    attended = jnp.concatenate([att_s[w].T for w in range(walkers)], axis=0).astype(BF16)
    mixed_out = jnp.dot(attended, w_out[...], preferred_element_type=F32)
    hidden_out = (h_s[...].astype(F32) + mixed_out).astype(BF16).astype(F32)
    spin_row = gsp[me].astype(F32)
    spin_col = jnp.broadcast_to(spin_row, (rows, rows)).T[:, 0:1]
    up_col = jnp.concatenate([spin_col] * walkers, axis=0) > 0.5
    up_lane = jnp.concatenate([spin_row] * walkers, axis=1) > 0.5
    split = jnp.concatenate(
        [jnp.where(up_col, 0.0, hidden_out), jnp.where(up_col, hidden_out, 0.0)], axis=1
    ).astype(BF16)
    hidden_t = hidden_out.T
    split_t = jnp.concatenate(
        [jnp.where(up_lane, 0.0, hidden_t), jnp.where(up_lane, hidden_t, 0.0)], axis=0
    ).astype(BF16)
    orbitals = target.shape[1]
    both_rows = 2 * width
    backward = None
    loss = jnp.zeros((1, LANES), F32)
    for c in range(orbitals // LANES):
        columns = slice(c * LANES, (c + 1) * LANES)
        w_piece = w_orb[:, columns]
        residual = jnp.dot(split, w_piece, preferred_element_type=F32) - target[
            :, columns
        ].astype(F32)
        loss = loss + jnp.sum(residual * residual, axis=0, keepdims=True)
        signal = residual.astype(BF16)
        total_ref[c * both_rows : (c + 1) * both_rows, :] = jnp.dot(
            split_t, signal, preferred_element_type=F32
        )
        term = lax.dot_general(signal, w_piece, NT, preferred_element_type=F32)
        backward = term if backward is None else backward + term
    chosen = jnp.where(up_col, backward[:, width:], backward[:, :width]).astype(BF16)
    base = orbitals // LANES * both_rows
    total_ref[base : base + width, :] = jnp.dot(att_t, chosen, preferred_element_type=F32)
    total_ref[base + width :, :] = jnp.zeros((total_ref.shape[0] - base - width, LANES), F32)
    total_ref[base + width : base + width + 1, :] = 0.5 * loss


def chunk_bounds(height):
    tiles = height // 8
    parts = min(CHUNKS, tiles)
    edges = [8 * (tiles * i // parts) for i in range(parts + 1)]
    return list(zip(edges[:-1], edges[1:]))


def reduce_kernel(
    pairs, walks, part, out, r1, r2, a2, r3, s1, v1, s2, v2, s3, v3, s4, v4, s5, v5, s6, v6
):
    elec = lax.axis_index("elec")
    wk = lax.axis_index("walk")
    core, y = lax.rem(elec, 2), elec // 2
    height = part.shape[3]
    bounds = chunk_bounds(height)
    mesh_id = pl.DeviceIdType.MESH
    partner = {"elec": y * 2 + 1 - core}

    def over_y(k):
        return {"elec": lax.rem(y + 1 + k, pairs) * 2 + core}

    def over_w(k):
        return {"walk": lax.rem(wk + 1 + k, walks)}

    barrier = pltpu.get_barrier_semaphore()
    peers = [partner] + [over_y(k) for k in range(pairs - 1)] + [over_w(k) for k in range(walks - 1)]
    for peer in peers:
        pl.semaphore_signal(barrier, inc=1, device_id=peer, device_id_type=mesh_id)
    pl.semaphore_wait(barrier, len(peers))

    def send(src, dst, ssem, rsem, peer):
        copy = pltpu.make_async_remote_copy(
            src_ref=src,
            dst_ref=dst,
            send_sem=ssem,
            recv_sem=rsem,
            device_id=peer,
            device_id_type=mesh_id,
        )
        copy.start()
        return copy

    flights = {}

    def step(stage, c):
        low, high = bounds[c]
        rng = pl.ds(low, high - low)
        if stage > 0:
            for copy in flights[stage - 1, c]:
                copy.wait_recv()
        if stage == 0:
            flights[stage, c] = [
                send(
                    part.at[1 - core, :, :, rng],
                    r1.at[:, :, rng],
                    s1.at[c],
                    v1.at[c],
                    partner,
                )
            ]
        elif stage == 1:
            r1[:, :, rng] = r1[:, :, rng] + part[core, :, :, rng]
            flights[stage, c] = [
                send(
                    r1.at[lax.rem(y + 1 + k, pairs), :, rng],
                    r2.at[k, :, rng],
                    s2.at[c, k],
                    v2.at[c, k],
                    over_y(k),
                )
                for k in range(pairs - 1)
            ]
        elif stage == 2:
            value = r1[y, :, rng]
            for k in range(pairs - 1):
                value = value + r2[k, :, rng]
            a2[:, rng] = value
            flights[stage, c] = [
                send(
                    a2.at[lax.rem(wk + 1 + k, walks), rng],
                    r3.at[k, rng],
                    s3.at[c, k],
                    v3.at[c, k],
                    over_w(k),
                )
                for k in range(walks - 1)
            ]
        elif stage == 3:
            value = a2[wk, rng]
            for k in range(walks - 1):
                value = value + r3[k, rng]
            out[core, y, wk, rng] = value
            here = out.at[core, y, wk, rng]
            flights[stage, c] = [
                send(here, here, s4.at[c, k], v4.at[c, k], over_w(k)) for k in range(walks - 1)
            ]
        elif stage == 4:
            here = out.at[core, y, :, rng]
            flights[stage, c] = [
                send(here, here, s5.at[c, k], v5.at[c, k], over_y(k)) for k in range(pairs - 1)
            ]
        elif stage == 5:
            here = out.at[core, :, :, rng]
            flights[stage, c] = [send(here, here, s6.at[c], v6.at[c], partner)]

    for t in range(len(bounds) + 6):
        for stage in reversed(range(7)):
            if 0 <= t - stage < len(bounds):
                step(stage, t - stage)
    for group in flights.values():
        for copy in group:
            copy.wait_send()


def local(
    elec_pos,
    atom_pos,
    atom_emb,
    spin_emb,
    spin,
    near_atoms,
    pair_list,
    pair_count,
    w_query,
    w_key,
    w_value,
    w_out,
    w_orb,
    target,
):
    walkers, rows = elec_pos.shape[1], elec_pos.shape[2]
    count, walks = lax.axis_size("elec"), lax.axis_size("walk")
    width, orbitals = w_query.shape[0], w_orb.shape[2]
    row_local = walkers * rows
    vmem = pl.BlockSpec(memory_space=VM)
    smem = pl.BlockSpec(memory_space=pltpu.SMEM)
    sem = pltpu.SemaphoreType.DMA
    gathered = pl.pallas_call(
        lambda *refs: gather_kernel(count, *refs),
        out_shape=(
            jax.ShapeDtypeStruct((count, ATOM_DEV, width), F32),
            jax.ShapeDtypeStruct((count, ATOM_DEV, 3), F32),
            jax.ShapeDtypeStruct((count, 3, walkers, rows), F32),
            jax.ShapeDtypeStruct((count, 1, rows), jnp.int32),
        ),
        in_specs=[vmem] * 4,
        out_specs=(vmem,) * 4,
        scratch_shapes=[sem((count - 1, 4)), sem((count - 1, 4))],
        compiler_params=pltpu.CompilerParams(collective_id=0, has_side_effects=True),
        name="gather_small",
    )(atom_emb, atom_pos, elec_pos, spin.reshape(1, rows))
    used = orbitals // LANES * 2 * width + width + 8
    devices = count * walks
    height = -(-used // (devices * 8)) * 8
    depth = rows // BLOCK * NEAR * SLOT
    part = pl.pallas_call(
        lambda *refs: compute_kernel(count, *refs),
        out_shape=jax.ShapeDtypeStruct((devices * height, LANES), F32),
        in_specs=[smem] * 3 + [vmem] * 11,
        out_specs=vmem,
        scratch_shapes=[
            VM((3, depth, 128), F32),
            VM((3, depth, width), F32),
            VM((walkers, rows, width), F32),
            VM((walkers, 3 * rows, width), BF16),
            VM((walkers, width, 3 * rows), BF16),
            VM((row_local, width), BF16),
            VM((3 * rows, 2 * rows), F32),
            VM((walkers, width, rows), F32),
        ],
        compiler_params=pltpu.CompilerParams(vmem_limit_bytes=40 * 1024 * 1024),
        name="local_step",
    )(
        near_atoms,
        pair_list,
        pair_count.reshape(-1, 1),
        *gathered,
        spin_emb,
        w_query,
        w_key,
        w_value,
        w_out,
        w_orb.reshape(2 * width, orbitals),
        target.reshape(row_local, orbitals),
    )
    pairs = count // 2
    chunks = len(chunk_bounds(height))
    reduced = pl.pallas_call(
        lambda *refs: reduce_kernel(pairs, walks, *refs),
        out_shape=jax.ShapeDtypeStruct((2, pairs, walks, height, LANES), F32),
        in_specs=[vmem],
        out_specs=vmem,
        scratch_shapes=[
            VM((pairs, walks, height, LANES), F32),
            VM((pairs - 1, walks, height, LANES), F32),
            VM((walks, height, LANES), F32),
            VM((walks - 1, height, LANES), F32),
            sem((chunks,)),
            sem((chunks,)),
            sem((chunks, pairs - 1)),
            sem((chunks, pairs - 1)),
            sem((chunks, walks - 1)),
            sem((chunks, walks - 1)),
            sem((chunks, walks - 1)),
            sem((chunks, walks - 1)),
            sem((chunks, pairs - 1)),
            sem((chunks, pairs - 1)),
            sem((chunks,)),
            sem((chunks,)),
        ],
        compiler_params=pltpu.CompilerParams(
            collective_id=1, has_side_effects=True, vmem_limit_bytes=40 * 1024 * 1024
        ),
        name="sum_all",
    )(part.reshape(2, pairs, walks, height, LANES))
    flat = reduced.reshape(devices * height, LANES)
    scale = F32(row_local * devices)
    base = orbitals // LANES * 2 * width
    grad_orb = (
        flat[:base]
        .reshape(orbitals // LANES, 2, width, LANES)
        .transpose(1, 2, 0, 3)
        .reshape(2, width, orbitals)
        / scale
    )
    grad_out = flat[base : base + width] / scale
    loss = jnp.sum(flat[base + width : base + width + 1], axis=1) / scale
    return (grad_orb, grad_out, loss)


def solution(mesh):
    in_specs = (
        P(None, ("parts", "walk"), "elec"),
        P(("parts", "elec"), None),
        P(("parts", "elec"), None),
        P(),
        P(("parts", "elec")),
        P("parts", None),
        P("parts", None),
        P("parts"),
        P(),
        P(),
        P(),
        P(),
        P(),
        P(("parts", "walk"), "elec", None),
    )
    out_specs = (P("parts", None, None), P("parts", None), P("parts"))
    return jax.shard_map(local, mesh=mesh, in_specs=in_specs, out_specs=out_specs, check_vma=False)
```

time: 198 us -> 93 us (0.47)
  Pallas kernels: 0 us -> 73.4 us
  waiting for transfers between devices: 63.9 us -> 0 us
  blocking collectives: 47.7 us -> 0 us
  matrix products: 26.4 us -> 0 us
  between operations: 17.6 us -> 2.46 us
  other arithmetic: 13.7 us -> 1.46 us
  local copies, waits for them, and re-layouts: 25.5 us -> 15.1 us
  starting transfers between devices: 2.44 us -> 0 us
    pallas_call x0 -> x3, Pallas kernels: none -> 73.4 us  [the longest x1 49.8 us: local(): pl.pallas_call(lambda *refs: reduce_kernel(pairs, walks, *refs), out_shap...]
    psum x1 -> x0, waiting for transfers between devices: 63.9 us -> none  [local(): lax.psum((orb_part, out_part, loss_part), ('elec', 'walk'))]
    psum x1 -> x0, blocking collectives: 35.5 us -> none  [local(): lax.psum((orb_part, out_part, loss_part), ('elec', 'walk'))]
    dot_general x17 -> x0, matrix products: 26.4 us -> none  [the longest x3 8.22 us: attend_piece(): jnp.einsum('wqhk,wkhd->wqhd', weights.astype(jnp.bfloat16), value_heads,...]
    all_gather x2 -> x0, blocking collectives: 12.1 us -> none  [the longest x1 6.28 us: local(): lax.all_gather(atom_pos, 'elec', axis=0, tiled=True)]
    gather x14 -> x0, local copies, waits for them, and re-layouts: 10.4 us -> none  [the longest x1 3.68 us: local(): sorted_target = jnp.take(target, by_spin, axis=1)]
    unnamed x32 -> x25, local copies, waits for them, and re-layouts: 4.51 us -> 12.8 us
    ppermute x4 -> x0, local copies, waits for them, and re-layouts: 4.48 us -> none  [shifted(): return lax.ppermute(block, axis, route)]
  transfers between devices with their start and end apart: 5 -> 0, of which waited for: 1 -> 0; matrix products, arithmetic and copies ran while one was open for 16% -> 0% of each run, Pallas kernels for 0% -> 0%
where the time goes in v1:
time: 93 us; the launch traced here: 92.4 us
  Pallas kernels  73.4 us (79%)
  local copies, waits for them, and re-layouts  15.1 us (16%)
  between operations  2.46 us (3%)
  other arithmetic  1.46 us (2%)
    pallas_call x1, Pallas kernels, local(): pl.pallas_call(lambda *refs: reduce_kernel(pairs, walks, *refs), out_shap...  49.8 us
    pallas_call x1, Pallas kernels, local(): pl.pallas_call(lambda *refs: compute_kernel(count, *refs), out_shape=jax....  16.1 us
    unnamed x25, local copies, waits for them, and re-layouts  12.8 us
    pallas_call x1, Pallas kernels, local(): pl.pallas_call(lambda *refs: gather_kernel(count, *refs), out_shape=(jax....  7.46 us

profile of v1, /device:TPU:0, one launch (start us, length us, event | category | flops | bytes accessed | tf_op | source)
XLA Modules:
  0.0 92.4 jit_solution(5551460211380549411)
XLA Ops:
  0.6 0.8 copy.18.refs_0_
  1.4 0.8 copy.19.refs_1_
  2.1 0.7 copy.20.refs_2_
  2.9 1.4 %copy.17.refs_1_ = f32[25,3]{1,0:T(8,128)} copy(f32[25,3]{0,1:T(4,128)} %param.15) | data formatting | bytes 600 | tf_op args[1]
  4.2 7.5 %gather_small.1 = (f32[4,25,256]{2,1,0:T(8,128)}, f32[4,25,3]{2,1,0:T(8,128)}, f32[4,3,4,128]{3,2,1,0:T(4,128)}, s32[4,1,128]{2,1,0:T(1,128)}) custom-call(f32[25,256]{1,0:T(8,128)} %refs_0_.2, f32[25,3]{1,0:T(8,128)} %copy.17.refs_1_, f32[3,4,128]{2,1,0:T(4,128)} %refs_2_.1, s32[1,128]{1,0:T(1,128)} %bitcast.20), custom_call_target="tpu_custom_call" | custom-call | tf_op jit(solution)/shard_map/gather_small/pallas_call | solution.py:355
  11.7 0.0 copy-start
  11.7 1.2 %copy-done = bf16[2,256,1024]{2,1,0:T(8,128)(2,1)S(1)} copy-done((bf16[2,256,1024]{2,1,0:T(8,128)(2,1)S(1)}, bf16[2,256,1024]{2,1,0:T(8,128)(2,1)}, u32[]{:S(2)}) %copy-start) | copy-done | bytes 1048600
  12.9 0.0 copy-start.1
  12.9 1.2 %copy-done.1 = bf16[4,128,1024]{2,1,0:T(8,128)(2,1)S(1)} copy-done((bf16[4,128,1024]{2,1,0:T(8,128)(2,1)S(1)}, bf16[4,128,1024]{2,1,0:T(8,128)(2,1)}, u32[]{:S(2)}) %copy-start.1) | copy-done | bytes 1048600
  14.2 0.9 copy-done.2
  15.1 0.9 copy-done.3
  16.0 0.9 copy-done.4
  16.9 0.9 copy-done.5
  17.8 0.9 copy-done.6
  18.7 0.8 copy-done.7
  19.5 0.7 copy-done.8
  20.3 0.7 copy-done.9
  20.9 0.7 copy-done.10
  21.6 16.1 %local_step.1 = f32[2432,256]{1,0:T(8,128)S(1)} custom-call(s32[8,2]{1,0:T(8,128)S(1)} %copy.18.refs_0_, s32[8,4]{1,0:T(8,128)S(1)} %copy.19.refs_1_, s32[8,1]{1,0:T(8,128)S(1)} %copy.20.refs_2_, f32[4,25,256]{2,1,0:T(8,128)S(1)} %copy-done.6, f32[4,25,3]{2,1,0:T(8,128)S(1)} %copy-done.7, f32[4,3,4,128]{3,2,1,0:T(4,128)S(1)} %copy-done.8, ...), custom_call_target="tpu_custom_call" | custom-call | tf_op jit(solution)/shard_map/local_step/pallas_call | solution.py:373
  37.7 49.8 %sum_all.1 = f32[2,2,4,152,256]{4,3,2,1,0:T(8,128)S(1)} custom-call(f32[2,2,4,152,256]{4,3,2,1,0:T(8,128)S(1)} %bitcast.12), custom_call_target="tpu_custom_call" | custom-call | tf_op jit(solution)/shard_map/sum_all/pallas_call | solution.py:405
  87.6 0.6 slice_reduce_fusion
  88.8 0.7 slice_multiply_fusion.1
  89.6 0.1 slice_multiply_fusion
  89.7 1.6 %copy.22 = f32[4,2,32,8,256]{4,3,0,2,1:T(8,128)} copy(f32[4,2,32,8,256]{4,3,2,1,0:T(8,128)S(1)} %bitcast.18) | data formatting | bytes 4194304 | tf_op jit(solution)/shard_map/div | solution.py:437
  (9 shorter events, 0.0 us)
Async XLA Ops:
  11.7 1.2 %copy-start = (bf16[2,256,1024]{2,1,0:T(8,128)(2,1)S(1)}, bf16[2,256,1024]{2,1,0:T(8,128)(2,1)}, u32[]{:S(2)}) copy-start(bf16[2,256,1024]{2,1,0:T(8,128)(2,1)} %param.26) | copy-start | bytes 3145732
  12.9 1.2 %copy-start.1 = (bf16[4,128,1024]{2,1,0:T(8,128)(2,1)S(1)}, bf16[4,128,1024]{2,1,0:T(8,128)(2,1)}, u32[]{:S(2)}) copy-start(bf16[4,128,1024]{2,1,0:T(8,128)(2,1)} %param.27) | copy-start | bytes 3145732
  14.2 0.9 copy-start.2
  15.1 0.9 copy-start.3
  16.0 0.9 copy-start.4
  16.9 0.9 copy-start.5
  17.8 0.9 copy-start.6
  18.7 0.8 copy-start.7
  19.5 0.7 copy-start.8
  20.3 0.7 copy-start.9
  20.9 0.7 copy-start.10

commit v2 on v1

v2 whole, which is shorter than its diff:
```python
import math

import jax
import jax.numpy as jnp
from jax import lax
from jax.experimental import pallas as pl
from jax.experimental.pallas import tpu as pltpu
from jax.sharding import PartitionSpec as P

HEADS = 16
BLOCK = 64
ATOM_DEV = 25
NEAR = 2
KMAX = 4
SLOT = 32
LANES = 256
CHUNKS = 8
F32 = jnp.float32
BF16 = jnp.bfloat16
VM = pltpu.VMEM
NT = (((1,), (1,)), ((), ()))


def compute_kernel(
    count,
    near,
    pairs,
    pair_n,
    emb,
    pos,
    epos,
    spin,
    *rest,
):
    outer, inner = rest[:7], rest[8:]
    total_ref = rest[7]
    gemb, gpos, gep, gsp = inner[:4]
    held = inner[4:11]
    spin_emb, w_query, w_key, w_value, w_out, w_orb, target = held
    send, recv, local_sem = inner[11:14]
    pstack, estack, e_s, q_s, k_s, vt_s, h_s, bias_s, att_s = inner[14:]
    me = lax.axis_index("elec")
    barrier = pltpu.get_barrier_semaphore()
    for k in range(count - 1):
        pl.semaphore_signal(
            barrier,
            inc=1,
            device_id={"elec": lax.rem(me + 1 + k, count)},
            device_id_type=pl.DeviceIdType.MESH,
        )
    small = ((emb, gemb), (pos, gpos), (epos, gep), (spin, gsp))
    own = [
        pltpu.make_async_copy(src, dst.at[me], local_sem.at[i])
        for i, (src, dst) in enumerate(small)
    ]
    loads = [
        pltpu.make_async_copy(src, dst, local_sem.at[4 + i])
        for i, (src, dst) in enumerate(zip(outer, held))
    ]
    for copy in own + loads:
        copy.start()
    pl.semaphore_wait(barrier, count - 1)
    copies = []
    for k in range(count - 1):
        for i, (src, dst) in enumerate(small):
            copy = pltpu.make_async_remote_copy(
                src_ref=src,
                dst_ref=dst.at[me],
                send_sem=send.at[k, i],
                recv_sem=recv.at[k, i],
                device_id={"elec": lax.rem(me + 1 + k, count)},
                device_id_type=pl.DeviceIdType.MESH,
            )
            copy.start()
            copies.append(copy)
    walkers, rows = gep.shape[2], gep.shape[3]
    width = w_query.shape[0]
    head = width // HEADS
    per_device = rows // BLOCK
    owners = (me, lax.rem(me + count - 1, count), lax.rem(me + 1, count))
    pstack[...] = jnp.zeros_like(pstack)
    estack[...] = jnp.zeros_like(estack)
    e_s[...] = jnp.zeros_like(e_s)
    depth = per_device * NEAR * SLOT
    row_id = lax.broadcasted_iota(jnp.int32, (rows, depth), 0)
    lane_id = lax.broadcasted_iota(jnp.int32, (rows, depth), 1)
    block_mask = (row_id // BLOCK) == (lane_id // (NEAR * SLOT))
    half_lane = lax.broadcasted_iota(jnp.int32, (BLOCK, 2 * rows), 1)
    for j, owner in enumerate(owners):
        for kb in range(per_device):
            key_block = owner * per_device + kb
            value = jnp.zeros((BLOCK, 2 * rows), F32)
            for p in range(per_device):
                query_block = me * per_device + p
                listed = None
                for slot in range(KMAX):
                    hit = jnp.logical_and(
                        pairs[slot, query_block] == key_block, slot < pair_n[0, query_block]
                    )
                    listed = hit if listed is None else jnp.logical_or(listed, hit)
                level = jnp.where(listed, 0.0, -1e30).astype(F32)
                value = jnp.where(half_lane % rows // BLOCK == p, level, value)
            start = j * rows + kb * BLOCK
            bias_s[start : start + BLOCK, :] = value
    for copy in own + loads[:4]:
        copy.wait()
    wv_t = w_value[...].astype(F32).T.astype(BF16)
    for copy in copies:
        copy.wait_recv()
    spin_cols = []
    for j, owner in enumerate(owners):
        for p in range(per_device):
            for n in range(NEAR):
                slot = p * NEAR + n
                group = near[n, owner * per_device + p]
                pstack[j, 0:3, slot * SLOT : slot * SLOT + ATOM_DEV] = gpos[group]
                estack[j, slot * SLOT : slot * SLOT + ATOM_DEV, :] = gemb[group]
        estack[j, ATOM_DEV : ATOM_DEV + 2, :] = spin_emb[...]
        electron = gep[owner]
        for axis in range(3):
            e_s[j, axis * walkers : (axis + 1) * walkers, :] = electron[axis]
        e_s[j, 3 * walkers : 3 * walkers + 1, :] = gsp[owner].astype(F32)
        columns = e_s[j].T
        up_one = columns[:, 3 * walkers : 3 * walkers + 1]
        spin_cols.append(up_one)
        pieces = []
        for w in range(walkers):
            distance = jnp.zeros((rows, depth), F32)
            for axis in range(3):
                at = axis * walkers + w
                spacing = columns[:, at : at + 1] - pstack[j, axis : axis + 1, :]
                distance = distance + spacing * spacing
            close = jnp.where(block_mask, 1.0 / (1.0 + distance), 0.0)
            close = jnp.where(lane_id == ATOM_DEV, 1.0 - up_one, close)
            close = jnp.where(lane_id == ATOM_DEV + 1, up_one, close)
            pieces.append(close)
        close_all = jnp.concatenate(pieces, axis=0)
        hidden = jnp.dot(
            close_all,
            estack[j],
            precision=lax.Precision.HIGHEST,
            preferred_element_type=F32,
        ).astype(BF16)
        keys = jnp.dot(hidden, w_key[...], preferred_element_type=F32).astype(BF16)
        values_t = lax.dot_general(wv_t, hidden, NT, preferred_element_type=F32).astype(BF16)
        for w in range(walkers):
            k_s[w, j * rows : (j + 1) * rows, :] = keys[w * rows : (w + 1) * rows]
            vt_s[w, :, j * rows : (j + 1) * rows] = values_t[:, w * rows : (w + 1) * rows]
        if j == 0:
            h_s[...] = hidden
            queries = jnp.dot(hidden, w_query[...], preferred_element_type=F32).astype(BF16)
            queries = queries.astype(F32) * (1.0 / math.sqrt(head))
            for w in range(walkers):
                q_s[w] = queries[w * rows : (w + 1) * rows]
    head_lane = lax.broadcasted_iota(jnp.int32, (rows, width), 1) // head

    def walker(w, carry):
        query = q_s[w]
        key = k_s[w]
        for pair in range(HEADS // 2):
            both = jnp.concatenate(
                [
                    jnp.where(head_lane == 2 * pair, query, 0.0),
                    jnp.where(head_lane == 2 * pair + 1, query, 0.0),
                ],
                axis=0,
            ).astype(BF16)
            scores = lax.dot_general(key, both, NT, preferred_element_type=F32) + bias_s[...]
            top = jnp.max(scores, axis=0, keepdims=True)
            weights = jnp.exp(scores - top)
            total = jnp.sum(weights, axis=0, keepdims=True)
            mixed = jnp.dot(
                vt_s[w, 2 * pair * head : 2 * (pair + 1) * head, :],
                weights.astype(BF16),
                preferred_element_type=F32,
            )
            mixed = mixed / total
            att_s[w, 2 * pair * head : (2 * pair + 1) * head, :] = mixed[:head, :rows]
            att_s[w, (2 * pair + 1) * head : 2 * (pair + 1) * head, :] = mixed[head:, rows:]
        return carry

    lax.fori_loop(0, walkers, walker, 0)
    for copy in loads[4:]:
        copy.wait()
    att_t = jnp.concatenate([att_s[w].astype(BF16) for w in range(walkers)], axis=1)
    attended = jnp.concatenate([att_s[w].T for w in range(walkers)], axis=0).astype(BF16)
    mixed_out = jnp.dot(attended, w_out[...], preferred_element_type=F32)
    hidden_out = (h_s[...].astype(F32) + mixed_out).astype(BF16).astype(F32)
    spin_row = gsp[me].astype(F32)
    spin_col = spin_cols[0]
    up_col = jnp.concatenate([spin_col] * walkers, axis=0) > 0.5
    up_lane = jnp.concatenate([spin_row] * walkers, axis=1) > 0.5
    split = jnp.concatenate(
        [jnp.where(up_col, 0.0, hidden_out), jnp.where(up_col, hidden_out, 0.0)], axis=1
    ).astype(BF16)
    hidden_t = hidden_out.T
    split_t = jnp.concatenate(
        [jnp.where(up_lane, 0.0, hidden_t), jnp.where(up_lane, hidden_t, 0.0)], axis=0
    ).astype(BF16)
    orbitals = target.shape[1]
    both_rows = 2 * width
    share = 1.0 / (walkers * rows * count * lax.axis_size("walk"))
    backward = None
    loss = jnp.zeros((1, LANES), F32)
    for c in range(orbitals // LANES):
        columns = slice(c * LANES, (c + 1) * LANES)
        w_piece = w_orb[:, columns]
        residual = jnp.dot(split, w_piece, preferred_element_type=F32) - target[
            :, columns
        ].astype(F32)
        loss = loss + jnp.sum(residual * residual, axis=0, keepdims=True)
        signal = residual.astype(BF16)
        total_ref[c * both_rows : (c + 1) * both_rows, :] = share * jnp.dot(
            split_t, signal, preferred_element_type=F32
        )
        term = lax.dot_general(signal, w_piece, NT, preferred_element_type=F32)
        backward = term if backward is None else backward + term
    chosen = jnp.where(up_col, backward[:, width:], backward[:, :width]).astype(BF16)
    base = orbitals // LANES * both_rows
    total_ref[base : base + width, :] = share * jnp.dot(
        att_t, chosen, preferred_element_type=F32
    )
    total_ref[base + width :, :] = jnp.zeros((total_ref.shape[0] - base - width, LANES), F32)
    total_ref[base + width : base + width + 1, :] = jnp.broadcast_to(
        (0.5 * share) * jnp.sum(loss, axis=1, keepdims=True), (1, LANES)
    )
    for copy in copies:
        copy.wait_send()


def chunk_bounds(height):
    tiles = height // 8
    parts = min(CHUNKS, tiles)
    edges = [8 * (tiles * i // parts) for i in range(parts + 1)]
    return list(zip(edges[:-1], edges[1:]))


def reduce_kernel(pairs, walks, part, out, r1, r2, a2, r3, r4, *sems):
    send_core, recv_core, send_y, recv_y, send_z, recv_z, send_c, recv_c, send_b, recv_b = sems[:10]
    send_y2, recv_y2, send_core2, recv_core2 = sems[10:]
    elec = lax.axis_index("elec")
    wk = lax.axis_index("walk")
    core, y = lax.rem(elec, 2), elec // 2
    bounds = chunk_bounds(part.shape[2])
    mesh_id = pl.DeviceIdType.MESH
    middle = walks // 2
    on_left = wk < middle
    level = jnp.where(on_left, wk, walks - 1 - wk)
    toward = jnp.where(on_left, 1, walks - 1)
    partner = {"elec": y * 2 + 1 - core}
    inward = {"walk": lax.rem(wk + toward, walks)}
    outward = {"walk": lax.rem(wk + walks - toward, walks)}

    def over_y(k):
        return {"elec": lax.rem(y + 1 + k, pairs) * 2 + core}

    barrier = pltpu.get_barrier_semaphore()
    peers = [partner, inward] + [over_y(k) for k in range(pairs - 1)]
    for peer in peers:
        pl.semaphore_signal(barrier, inc=1, device_id=peer, device_id_type=mesh_id)

    @pl.when(level > 0)
    def _():
        pl.semaphore_signal(barrier, inc=1, device_id=outward, device_id_type=mesh_id)

    pl.semaphore_wait(barrier, len(peers) + jnp.where(level > 0, 1, 0))

    def route(src, dst, ssem, rsem, peer):
        return pltpu.make_async_remote_copy(
            src_ref=src,
            dst_ref=dst,
            send_sem=ssem,
            recv_sem=rsem,
            device_id=peer,
            device_id_type=mesh_id,
        )

    def copies(c):
        low, high = bounds[c]
        rng = pl.ds(low, high - low)
        whole = out.at[core, :, rng]
        mine = out.at[core, y, rng]
        return dict(
            core=route(
                part.at[1 - core, :, rng], r1.at[:, rng], send_core.at[c], recv_core.at[c], partner
            ),
            y=[
                route(
                    r1.at[lax.rem(y + 1 + k, pairs), rng],
                    r2.at[k, rng],
                    send_y.at[c, k],
                    recv_y.at[c, k],
                    over_y(k),
                )
                for k in range(pairs - 1)
            ],
            z=route(a2.at[rng], r3.at[rng], send_z.at[c], recv_z.at[c], inward),
            c=route(a2.at[rng], r4.at[rng], send_c.at[c], recv_c.at[c], inward),
            b=route(mine, mine, send_b.at[c], recv_b.at[c], outward),
            y2=[
                route(mine, mine, send_y2.at[c, k], recv_y2.at[c, k], over_y(k))
                for k in range(pairs - 1)
            ],
            core2=route(whole, whole, send_core2.at[c], recv_core2.at[c], partner),
        )

    flights = [copies(c) for c in range(len(bounds))]
    inner_level = middle - 1

    def step(stage, c):
        flight = flights[c]
        low, high = bounds[c]
        rng = pl.ds(low, high - low)
        if stage == 0:
            for copy in flight["y"]:
                copy.wait_recv()
            value = r1[y, rng]
            for k in range(pairs - 1):
                value = value + r2[k, rng]
            a2[rng] = value

            @pl.when(jnp.logical_and(level == 0, inner_level > 0))
            def _():
                flight["z"].start()
        elif stage < middle:

            @pl.when(level == stage)
            def _():
                flight["z"].wait_recv()
                a2[rng] = a2[rng] + r3[rng]
                if stage < inner_level:
                    flight["z"].start()
        if stage == inner_level:

            @pl.when(level == inner_level)
            def _():
                flight["c"].start()

        back = stage - middle
        if back == 0:

            @pl.when(level == inner_level)
            def _():
                flight["c"].wait_recv()
                out[core, y, rng] = a2[rng] + r4[rng]
                if inner_level > 0:
                    flight["b"].start()
                for copy in flight["y2"]:
                    copy.start()
        elif 0 < back < middle:

            @pl.when(level == inner_level - back)
            def _():
                flight["b"].wait_recv()
                if back < inner_level:
                    flight["b"].start()
                for copy in flight["y2"]:
                    copy.start()

        if back == middle:
            for copy in flight["y2"]:
                copy.wait_recv()
            flight["core2"].start()
        elif back == middle + 1:
            flight["core2"].wait_recv()

    for flight in flights:
        flight["core"].start()
    for flight, (low, high) in zip(flights, bounds):
        rng = pl.ds(low, high - low)
        flight["core"].wait_recv()
        r1[:, rng] = r1[:, rng] + part[core, :, rng]
        for copy in flight["y"]:
            copy.start()
    stages = 2 * middle + 2
    for t in range(len(bounds) + stages - 1):
        for stage in reversed(range(stages)):
            if 0 <= t - stage < len(bounds):
                step(stage, t - stage)
    for flight in flights:
        for copy in [flight["core"], flight["core2"]] + flight["y"] + flight["y2"]:
            copy.wait_send()

        @pl.when(level < inner_level)
        def _():
            flight["z"].wait_send()

        @pl.when(level == inner_level)
        def _():
            flight["c"].wait_send()

        @pl.when(level > 0)
        def _():
            flight["b"].wait_send()


def local(
    elec_pos,
    atom_pos,
    atom_emb,
    spin_emb,
    spin,
    near_atoms,
    pair_list,
    pair_count,
    w_query,
    w_key,
    w_value,
    w_out,
    w_orb,
    target,
):
    walkers, rows = elec_pos.shape[1], elec_pos.shape[2]
    count, walks = lax.axis_size("elec"), lax.axis_size("walk")
    width, orbitals = w_query.shape[0], w_orb.shape[2]
    row_local = walkers * rows
    vmem = pl.BlockSpec(memory_space=VM)
    smem = pl.BlockSpec(memory_space=pltpu.SMEM)
    sem = pltpu.SemaphoreType.DMA
    hbm = pl.BlockSpec(memory_space=pltpu.HBM)
    used = orbitals // LANES * 2 * width + width + 8
    height = -(-used // (count * 8)) * 8
    depth = rows // BLOCK * NEAR * SLOT
    part = pl.pallas_call(
        lambda *refs: compute_kernel(count, *refs),
        out_shape=jax.ShapeDtypeStruct((count * height, LANES), F32),
        in_specs=[smem] * 3 + [hbm] * 11,
        out_specs=vmem,
        scratch_shapes=[
            VM((count, ATOM_DEV, width), F32),
            VM((count, 3, ATOM_DEV), F32),
            VM((count, 3, walkers, rows), F32),
            VM((count, 1, rows), jnp.int32),
            VM((2, width), F32),
            VM((width, width), BF16),
            VM((width, width), BF16),
            VM((width, width), BF16),
            VM((width, width), BF16),
            VM((2 * width, orbitals), BF16),
            VM((row_local, orbitals), BF16),
            sem((count - 1, 4)),
            sem((count - 1, 4)),
            sem((11,)),
            VM((3, 8, depth), F32),
            VM((3, depth, width), F32),
            VM((3, rows, rows), F32),
            VM((walkers, rows, width), F32),
            VM((walkers, 3 * rows, width), BF16),
            VM((walkers, width, 3 * rows), BF16),
            VM((row_local, width), BF16),
            VM((3 * rows, 2 * rows), F32),
            VM((walkers, width, rows), F32),
        ],
        compiler_params=pltpu.CompilerParams(
            collective_id=0, has_side_effects=True, vmem_limit_bytes=40 * 1024 * 1024
        ),
        name="local_step",
    )(
        near_atoms.T,
        pair_list.T,
        pair_count.reshape(1, -1),
        atom_emb,
        atom_pos.T,
        elec_pos,
        spin.reshape(1, rows),
        spin_emb,
        w_query,
        w_key,
        w_value,
        w_out,
        w_orb.reshape(2 * width, orbitals),
        target.reshape(row_local, orbitals),
    )
    pairs = count // 2
    chunks = len(chunk_bounds(height))
    one, many = sem((chunks,)), sem((chunks, pairs - 1))
    reduced = pl.pallas_call(
        lambda *refs: reduce_kernel(pairs, walks, *refs),
        out_shape=jax.ShapeDtypeStruct((2, pairs, height, LANES), F32),
        in_specs=[vmem],
        out_specs=vmem,
        scratch_shapes=[
            VM((pairs, height, LANES), F32),
            VM((pairs - 1, height, LANES), F32),
            VM((height, LANES), F32),
            VM((height, LANES), F32),
            VM((height, LANES), F32),
        ]
        + [one] * 2
        + [many] * 2
        + [one] * 6
        + [many] * 2
        + [one] * 2,
        compiler_params=pltpu.CompilerParams(
            collective_id=1, has_side_effects=True, vmem_limit_bytes=40 * 1024 * 1024
        ),
        name="sum_all",
    )(part.reshape(2, pairs, height, LANES))
    flat = reduced.reshape(count * height, LANES)
    base = orbitals // LANES * 2 * width
    grad_orb = (
        flat[:base]
        .reshape(orbitals // LANES, 2, width, LANES)
        .transpose(1, 2, 0, 3)
        .reshape(2, width, orbitals)
    )
    grad_out = flat[base : base + width]
    loss = flat[base + width, :1]
    return (grad_orb, grad_out, loss)


def solution(mesh):
    in_specs = (
        P(None, ("parts", "walk"), "elec"),
        P(("parts", "elec"), None),
        P(("parts", "elec"), None),
        P(),
        P(("parts", "elec")),
        P("parts", None),
        P("parts", None),
        P("parts"),
        P(),
        P(),
        P(),
        P(),
        P(),
        P(("parts", "walk"), "elec", None),
    )
    out_specs = (P("parts", None, None), P("parts", None), P("parts"))
    return jax.shard_map(local, mesh=mesh, in_specs=in_specs, out_specs=out_specs, check_vma=False)
```

time: 93 us -> 88.2 us (0.948)
  between operations: 2.46 us -> 0.68 us
  other arithmetic: 1.46 us -> 0 us
    pallas_call x1 -> x0, Pallas kernels: 7.46 us -> none  [local(): pl.pallas_call(lambda *refs: gather_kernel(count, *refs), out_shape=(jax....]
    pallas_call x1, Pallas kernels: 16.1 us -> 22.3 us  [local(): pl.pallas_call(lambda *refs: compute_kernel(count, *refs), out_shape=jax....]
    div x1 -> x0, local copies, waits for them, and re-layouts: 1.58 us -> none  [local(): flat[:base].reshape(orbitals // LANES, 2, width, LANES)]
    slice x0 -> x3, local copies, waits for them, and re-layouts: none -> 1.37 us  [the longest x1 0.72 us: local(): grad_out = flat[base:base + width]]
    unnamed x25 -> x28, local copies, waits for them, and re-layouts: 12.8 us -> 11.5 us
where the time goes in v2:
time: 88.2 us; the launch traced here: 87.7 us
  Pallas kernels  72.6 us (82%)
  local copies, waits for them, and re-layouts  14.5 us (16%)
    pallas_call x1, Pallas kernels, local(): pl.pallas_call(lambda *refs: reduce_kernel(pairs, walks, *refs), out_shap...  50.3 us
    pallas_call x1, Pallas kernels, local(): pl.pallas_call(lambda *refs: compute_kernel(count, *refs), out_shape=jax....  22.3 us
    unnamed x28, local copies, waits for them, and re-layouts  11.5 us

profile of v2, /device:TPU:0, one launch (start us, length us, event | category | flops | bytes accessed | tf_op | source)
XLA Modules:
  0.0 87.7 jit_solution(10309084089050587282)
XLA Ops:
  0.6 0.0 copy-start
  0.6 1.2 %copy-done = bf16[2,256,1024]{2,1,0:T(8,128)(2,1)S(1)} copy-done((bf16[2,256,1024]{2,1,0:T(8,128)(2,1)S(1)}, bf16[2,256,1024]{2,1,0:T(8,128)(2,1)}, u32[]{:S(2)}) %copy-start) | copy-done | bytes 1048600
  1.9 0.0 copy-start.1
  1.9 1.2 %copy-done.1 = bf16[4,128,1024]{2,1,0:T(8,128)(2,1)S(1)} copy-done((bf16[4,128,1024]{2,1,0:T(8,128)(2,1)S(1)}, bf16[4,128,1024]{2,1,0:T(8,128)(2,1)}, u32[]{:S(2)}) %copy-start.1) | copy-done | bytes 1048600
  3.1 0.0 copy-start.2
  3.1 0.9 %copy-done.2 = bf16[256,256]{1,0:T(8,128)(2,1)S(1)} copy-done((bf16[256,256]{1,0:T(8,128)(2,1)S(1)}, bf16[256,256]{1,0:T(8,128)(2,1)}, u32[]{:S(2)}) %copy-start.2) | copy-done | bytes 131096
  4.0 0.0 copy-start.3
  4.0 0.9 %copy-done.3 = bf16[256,256]{1,0:T(8,128)(2,1)S(1)} copy-done((bf16[256,256]{1,0:T(8,128)(2,1)S(1)}, bf16[256,256]{1,0:T(8,128)(2,1)}, u32[]{:S(2)}) %copy-start.3) | copy-done | bytes 131096
  4.9 0.9 %copy-done.4 = bf16[256,256]{1,0:T(8,128)(2,1)S(1)} copy-done((bf16[256,256]{1,0:T(8,128)(2,1)S(1)}, bf16[256,256]{1,0:T(8,128)(2,1)}, u32[]{:S(2)}) %copy-start.4) | copy-done | bytes 131096
  5.8 0.9 %copy-done.5 = bf16[256,256]{1,0:T(8,128)(2,1)S(1)} copy-done((bf16[256,256]{1,0:T(8,128)(2,1)S(1)}, bf16[256,256]{1,0:T(8,128)(2,1)}, u32[]{:S(2)}) %copy-start.5) | copy-done | bytes 131096
  6.7 0.8 copy-done.6
  7.5 0.7 copy-done.7
  8.2 0.7 copy-done.8
  8.8 0.7 copy-done.9
  9.5 0.7 copy-done.10
  10.2 0.7 copy-done.11
  10.9 0.7 copy-done.12
  11.5 0.7 copy-done.13
  12.2 22.3 %local_step.1 = f32[2336,256]{1,0:T(8,128)S(1)} custom-call(s32[2,8]{1,0:T(2,128)S(1)} %bitcast.23, s32[4,8]{1,0:T(4,128)S(1)} %bitcast.21, s32[1,8]{1,0:T(1,128)S(1)} %bitcast.24, f32[25,256]{1,0:T(8,128)S(1)} %copy-done.6, f32[3,25]{1,0:T(4,128)S(1)} %bitcast.22, f32[3,4,128]{2,1,0:T(4,128)S(1)} %copy-done.7, s32[1,128]{1,0:T(1,128)S(1)} %bitcast.25, ...), custom_call_target="tpu_custom_call" | custom-call | tf_op jit(solution)/shard_map/local_step/pallas_call | solution.py:424
  34.5 50.3 %sum_all.1 = f32[2,2,584,256]{3,2,1,0:T(8,128)S(1)} custom-call(f32[2,2,584,256]{3,2,1,0:T(8,128)S(1)} %bitcast.15), custom_call_target="tpu_custom_call" | custom-call | tf_op jit(solution)/shard_map/sum_all/pallas_call | solution.py:477
  84.8 0.5 slice.14
  85.3 0.7 slice.13
  86.0 0.1 slice.12
  86.1 1.6 %copy.18 = f32[4,2,32,8,256]{4,3,0,2,1:T(8,128)} copy(f32[4,2,32,8,256]{4,3,2,1,0:T(8,128)S(1)} %bitcast.26) | data formatting | bytes 4194304 | tf_op jit(solution)/shard_map/reshape | solution.py:505
  (10 shorter events, 0.0 us)
Async XLA Ops:
  0.6 1.2 %copy-start = (bf16[2,256,1024]{2,1,0:T(8,128)(2,1)S(1)}, bf16[2,256,1024]{2,1,0:T(8,128)(2,1)}, u32[]{:S(2)}) copy-start(bf16[2,256,1024]{2,1,0:T(8,128)(2,1)} %param.26) | copy-start | bytes 3145732
  1.9 1.2 %copy-start.1 = (bf16[4,128,1024]{2,1,0:T(8,128)(2,1)S(1)}, bf16[4,128,1024]{2,1,0:T(8,128)(2,1)}, u32[]{:S(2)}) copy-start(bf16[4,128,1024]{2,1,0:T(8,128)(2,1)} %param.27) | copy-start | bytes 3145732
  3.1 0.9 %copy-start.2 = (bf16[256,256]{1,0:T(8,128)(2,1)S(1)}, bf16[256,256]{1,0:T(8,128)(2,1)}, u32[]{:S(2)}) copy-start(bf16[256,256]{1,0:T(8,128)(2,1)} %refs_8_.1) | copy-start | bytes 393220
  4.0 0.9 %copy-start.3 = (bf16[256,256]{1,0:T(8,128)(2,1)S(1)}, bf16[256,256]{1,0:T(8,128)(2,1)}, u32[]{:S(2)}) copy-start(bf16[256,256]{1,0:T(8,128)(2,1)} %refs_9_.1) | copy-start | bytes 393220
  4.9 0.9 %copy-start.4 = (bf16[256,256]{1,0:T(8,128)(2,1)S(1)}, bf16[256,256]{1,0:T(8,128)(2,1)}, u32[]{:S(2)}) copy-start(bf16[256,256]{1,0:T(8,128)(2,1)} %refs_10_.1) | copy-start | bytes 393220
  5.8 0.9 %copy-start.5 = (bf16[256,256]{1,0:T(8,128)(2,1)S(1)}, bf16[256,256]{1,0:T(8,128)(2,1)}, u32[]{:S(2)}) copy-start(bf16[256,256]{1,0:T(8,128)(2,1)} %refs_11_.1) | copy-start | bytes 393220
  6.7 0.8 copy-start.6
  7.5 0.7 copy-start.7
  8.2 0.7 copy-start.8
  8.8 0.7 copy-start.9
  9.5 0.7 copy-start.10
  10.2 0.7 copy-start.11
  10.9 0.7 copy-start.12
  11.5 0.7 copy-start.13

commit v3 on v2

--- a/solution.py
+++ b/solution.py
@@ -14,15 +14,183 @@
 KMAX = 4
 SLOT = 32
 LANES = 256
-CHUNKS = 8
+LAG = 2
+VMEM_MIB = 62
 F32 = jnp.float32
 BF16 = jnp.bfloat16
 VM = pltpu.VMEM
 NT = (((1,), (1,)), ((), ()))
 
 
-def compute_kernel(
+def chunk_bounds(piece, extra, columns):
+    half = piece // 2
+    edges = [(i * half, (i + 1) * half) for i in range(2 * columns)]
+    return edges + [(piece * columns, piece * columns + extra)]
+
+
+def make_steps(pairs, walks, bounds, part, out, r1, r2, a2, r3, r4, *sems):
+    send_core, recv_core, send_y, recv_y, send_z, recv_z, send_c, recv_c, send_b, recv_b = sems[:10]
+    send_y2, recv_y2, send_core2, recv_core2 = sems[10:]
+    elec = lax.axis_index("elec")
+    wk = lax.axis_index("walk")
+    core, y = lax.rem(elec, 2), elec // 2
+    mesh_id = pl.DeviceIdType.MESH
+    middle = walks // 2
+    on_left = wk < middle
+    level = jnp.where(on_left, wk, walks - 1 - wk)
+    toward = jnp.where(on_left, 1, walks - 1)
+    partner = {"elec": y * 2 + 1 - core}
+    inward = {"walk": lax.rem(wk + toward, walks)}
+    outward = {"walk": lax.rem(wk + walks - toward, walks)}
+
+    def over_y(k):
+        return {"elec": lax.rem(y + 1 + k, pairs) * 2 + core}
+
+    def route(src, dst, ssem, rsem, peer):
+        return pltpu.make_async_remote_copy(
+            src_ref=src,
+            dst_ref=dst,
+            send_sem=ssem,
+            recv_sem=rsem,
+            device_id=peer,
+            device_id_type=mesh_id,
+        )
+
+    def copies(c):
+        low, high = bounds[c]
+        rng = pl.ds(low, high - low)
+        whole = out.at[core, :, rng]
+        mine = out.at[core, y, rng]
+        return dict(
+            core=route(
+                part.at[1 - core, :, rng], r1.at[:, rng], send_core.at[c], recv_core.at[c], partner
+            ),
+            y=[
+                route(
+                    r1.at[lax.rem(y + 1 + k, pairs), rng],
+                    r2.at[k, rng],
+                    send_y.at[c, k],
+                    recv_y.at[c, k],
+                    over_y(k),
+                )
+                for k in range(pairs - 1)
+            ],
+            z=route(a2.at[rng], r3.at[rng], send_z.at[c], recv_z.at[c], inward),
+            c=route(a2.at[rng], r4.at[rng], send_c.at[c], recv_c.at[c], inward),
+            b=route(mine, mine, send_b.at[c], recv_b.at[c], outward),
+            y2=[
+                route(mine, mine, send_y2.at[c, k], recv_y2.at[c, k], over_y(k))
+                for k in range(pairs - 1)
+            ],
+            core2=route(whole, whole, send_core2.at[c], recv_core2.at[c], partner),
+        )
+
+    flights = [copies(c) for c in range(len(bounds))]
+    inner_level = middle - 1
+
+    def step(stage, c):
+        flight = flights[c]
+        low, high = bounds[c]
+        rng = pl.ds(low, high - low)
+        if stage == 0:
+            for copy in flight["y"]:
+                copy.wait_recv()
+            value = r1[y, rng]
+            for k in range(pairs - 1):
+                value = value + r2[k, rng]
+            a2[rng] = value
+
+            @pl.when(jnp.logical_and(level == 0, inner_level > 0))
+            def _():
+                flight["z"].start()
+        elif stage < middle:
+
+            @pl.when(level == stage)
+            def _():
+                flight["z"].wait_recv()
+                a2[rng] = a2[rng] + r3[rng]
+                if stage < inner_level:
+                    flight["z"].start()
+        if stage == inner_level:
+
+            @pl.when(level == inner_level)
+            def _():
+                flight["c"].start()
+
+        back = stage - middle
+        if back == 0:
+
+            @pl.when(level == inner_level)
+            def _():
+                flight["c"].wait_recv()
+                out[core, y, rng] = a2[rng] + r4[rng]
+                if inner_level > 0:
+                    flight["b"].start()
+                for copy in flight["y2"]:
+                    copy.start()
+        elif 0 < back < middle:
+
+            @pl.when(level == inner_level - back)
+            def _():
+                flight["b"].wait_recv()
+                if back < inner_level:
+                    flight["b"].start()
+                for copy in flight["y2"]:
+                    copy.start()
+
+        if back == middle:
+            for copy in flight["y2"]:
+                copy.wait_recv()
+            flight["core2"].start()
+        elif back == middle + 1:
+            flight["core2"].wait_recv()
+
+    def begin(c):
+        flights[c]["core"].start()
+
+    def pair_done(c):
+        low, high = bounds[c]
+        rng = pl.ds(low, high - low)
+        flights[c]["core"].wait_recv()
+        r1[:, rng] = r1[:, rng] + part[core, :, rng]
+        for copy in flights[c]["y"]:
+            copy.start()
+
+    stages = 2 * middle + 2
+
+    def advance(t):
+        for stage in reversed(range(stages)):
+            c = t - LAG * stage - LAG
+            if 0 <= c < len(bounds):
+                step(stage, c)
+        if t < len(bounds):
+            pair_done(t)
+
+    total_steps = len(bounds) + LAG * stages
+
+    def drain():
+        for flight in flights:
+            for copy in [flight["core"], flight["core2"]] + flight["y"] + flight["y2"]:
+                copy.wait_send()
+
+            @pl.when(level < inner_level)
+            def _():
+                flight["z"].wait_send()
+
+            @pl.when(level == inner_level)
+            def _():
+                flight["c"].wait_send()
+
+            @pl.when(level > 0)
+            def _():
+                flight["b"].wait_send()
+
+    return begin, advance, drain, total_steps
+
+
+def step_kernel(
     count,
+    walks,
     near,
     pairs,
     pair_n,
@@ -33,12 +201,12 @@
     *rest,
 ):
     outer, inner = rest[:7], rest[8:]
-    total_ref = rest[7]
+    out = rest[7]
     gemb, gpos, gep, gsp = inner[:4]
     held = inner[4:11]
     spin_emb, w_query, w_key, w_value, w_out, w_orb, target = held
     send, recv, local_sem = inner[11:14]
-    pstack, estack, e_s, q_s, k_s, vt_s, h_s, bias_s, att_s = inner[14:]
+    pstack, estack, e_s, q_s, k_s, vt_s, h_s, bias_s, att_s, part = inner[14:24]
     me = lax.axis_index("elec")
     barrier = pltpu.get_barrier_semaphore()
     for k in range(count - 1):
@@ -48,6 +216,27 @@
             device_id={"elec": lax.rem(me + 1 + k, count)},
             device_id_type=pl.DeviceIdType.MESH,
         )
+    wk = lax.axis_index("walk")
+
+    @pl.when(wk > 0)
+    def _():
+        pl.semaphore_signal(
+            barrier,
+            inc=1,
+            device_id={"walk": lax.rem(wk + walks - 1, walks)},
+            device_id_type=pl.DeviceIdType.MESH,
+        )
+
+    @pl.when(wk < walks - 1)
+    def _():
+        pl.semaphore_signal(
+            barrier,
+            inc=1,
+            device_id={"walk": lax.rem(wk + 1, walks)},
+            device_id_type=pl.DeviceIdType.MESH,
+        )
+
+    ends = jnp.where(wk > 0, 1, 0) + jnp.where(wk < walks - 1, 1, 0)
     small = ((emb, gemb), (pos, gpos), (epos, gep), (spin, gsp))
     own = [
         pltpu.make_async_copy(src, dst.at[me], local_sem.at[i])
@@ -59,7 +248,7 @@
     ]
     for copy in own + loads:
         copy.start()
-    pl.semaphore_wait(barrier, count - 1)
+    pl.semaphore_wait(barrier, count - 1 + ends)
     copies = []
     for k in range(count - 1):
         for i, (src, dst) in enumerate(small):
@@ -199,6 +388,15 @@
     ).astype(BF16)
     orbitals = target.shape[1]
     both_rows = 2 * width
+    pairs = count // 2
+    piece = both_rows // count
+    tail = width // count
+    columns_total = orbitals // LANES
+    bounds = chunk_bounds(piece, tail + 8, columns_total)
+    begin, advance, drain, total_steps = make_steps(
+        pairs, walks, bounds, part, out, *inner[24:]
+    )
+    moved = 0
     share = 1.0 / (walkers * rows * count * lax.axis_size("walk"))
     backward = None
     loss = jnp.zeros((1, LANES), F32)
@@ -210,188 +408,32 @@
         ].astype(F32)
         loss = loss + jnp.sum(residual * residual, axis=0, keepdims=True)
         signal = residual.astype(BF16)
-        total_ref[c * both_rows : (c + 1) * both_rows, :] = share * jnp.dot(
-            split_t, signal, preferred_element_type=F32
-        )
+        grad = share * jnp.dot(split_t, signal, preferred_element_type=F32)
+        for q in range(count):
+            part[q // pairs, q % pairs, c * piece : (c + 1) * piece, :] = grad[
+                q * piece : (q + 1) * piece
+            ]
+        begin(2 * c)
+        begin(2 * c + 1)
+        if c > 0 and moved < 2:
+            advance(moved)
+            moved = moved + 1
         term = lax.dot_general(signal, w_piece, NT, preferred_element_type=F32)
         backward = term if backward is None else backward + term
     chosen = jnp.where(up_col, backward[:, width:], backward[:, :width]).astype(BF16)
-    base = orbitals // LANES * both_rows
-    total_ref[base : base + width, :] = share * jnp.dot(
-        att_t, chosen, preferred_element_type=F32
-    )
-    total_ref[base + width :, :] = jnp.zeros((total_ref.shape[0] - base - width, LANES), F32)
-    total_ref[base + width : base + width + 1, :] = jnp.broadcast_to(
-        (0.5 * share) * jnp.sum(loss, axis=1, keepdims=True), (1, LANES)
-    )
+    grad = share * jnp.dot(att_t, chosen, preferred_element_type=F32)
+    spread = (0.5 * share) * jnp.sum(loss, axis=1, keepdims=True)
+    base = columns_total * piece
+    for q in range(count):
+        here = part.at[q // pairs, q % pairs]
+        here[base : base + tail, :] = grad[q * tail : (q + 1) * tail]
+        here[base + tail : base + tail + 8, :] = jnp.broadcast_to(spread, (8, LANES))
+    begin(len(bounds) - 1)
+    for t in range(moved, total_steps):
+        advance(t)
+    drain()
     for copy in copies:
         copy.wait_send()
-
-
-def chunk_bounds(height):
-    tiles = height // 8
-    parts = min(CHUNKS, tiles)
-    edges = [8 * (tiles * i // parts) for i in range(parts + 1)]
-    return list(zip(edges[:-1], edges[1:]))
-
-
-def reduce_kernel(pairs, walks, part, out, r1, r2, a2, r3, r4, *sems):
-    send_core, recv_core, send_y, recv_y, send_z, recv_z, send_c, recv_c, send_b, recv_b = sems[:10]
-    send_y2, recv_y2, send_core2, recv_core2 = sems[10:]
-    elec = lax.axis_index("elec")
-    wk = lax.axis_index("walk")
-    core, y = lax.rem(elec, 2), elec // 2
-    bounds = chunk_bounds(part.shape[2])
-    mesh_id = pl.DeviceIdType.MESH
-    middle = walks // 2
-    on_left = wk < middle
-    level = jnp.where(on_left, wk, walks - 1 - wk)
-    toward = jnp.where(on_left, 1, walks - 1)
-    partner = {"elec": y * 2 + 1 - core}
-    inward = {"walk": lax.rem(wk + toward, walks)}
-    outward = {"walk": lax.rem(wk + walks - toward, walks)}
-
-    def over_y(k):
-        return {"elec": lax.rem(y + 1 + k, pairs) * 2 + core}
-
-    barrier = pltpu.get_barrier_semaphore()
-    peers = [partner, inward] + [over_y(k) for k in range(pairs - 1)]
-    for peer in peers:
-        pl.semaphore_signal(barrier, inc=1, device_id=peer, device_id_type=mesh_id)
-
-    @pl.when(level > 0)
-    def _():
-        pl.semaphore_signal(barrier, inc=1, device_id=outward, device_id_type=mesh_id)
-
-    pl.semaphore_wait(barrier, len(peers) + jnp.where(level > 0, 1, 0))
-
-    def route(src, dst, ssem, rsem, peer):
-        return pltpu.make_async_remote_copy(
-            src_ref=src,
-            dst_ref=dst,
-            send_sem=ssem,
-            recv_sem=rsem,
-            device_id=peer,
-            device_id_type=mesh_id,
-        )
-
-    def copies(c):
-        low, high = bounds[c]
-        rng = pl.ds(low, high - low)
-        whole = out.at[core, :, rng]
-        mine = out.at[core, y, rng]
-        return dict(
-            core=route(
-                part.at[1 - core, :, rng], r1.at[:, rng], send_core.at[c], recv_core.at[c], partner
-            ),
-            y=[
-                route(
-                    r1.at[lax.rem(y + 1 + k, pairs), rng],
-                    r2.at[k, rng],
-                    send_y.at[c, k],
-                    recv_y.at[c, k],
-                    over_y(k),
-                )
-                for k in range(pairs - 1)
-            ],
-            z=route(a2.at[rng], r3.at[rng], send_z.at[c], recv_z.at[c], inward),
-            c=route(a2.at[rng], r4.at[rng], send_c.at[c], recv_c.at[c], inward),
-            b=route(mine, mine, send_b.at[c], recv_b.at[c], outward),
-            y2=[
-                route(mine, mine, send_y2.at[c, k], recv_y2.at[c, k], over_y(k))
-                for k in range(pairs - 1)
-            ],
-            core2=route(whole, whole, send_core2.at[c], recv_core2.at[c], partner),
-        )
-
-    flights = [copies(c) for c in range(len(bounds))]
-    inner_level = middle - 1
-
-    def step(stage, c):
-        flight = flights[c]
-        low, high = bounds[c]
-        rng = pl.ds(low, high - low)
-        if stage == 0:
-            for copy in flight["y"]:
-                copy.wait_recv()
-            value = r1[y, rng]
-            for k in range(pairs - 1):
-                value = value + r2[k, rng]
-            a2[rng] = value
-
-            @pl.when(jnp.logical_and(level == 0, inner_level > 0))
-            def _():
-                flight["z"].start()
-        elif stage < middle:
-
-            @pl.when(level == stage)
-            def _():
-                flight["z"].wait_recv()
-                a2[rng] = a2[rng] + r3[rng]
-                if stage < inner_level:
-                    flight["z"].start()
-        if stage == inner_level:
-
-            @pl.when(level == inner_level)
-            def _():
-                flight["c"].start()
-
-        back = stage - middle
-        if back == 0:
-
-            @pl.when(level == inner_level)
-            def _():
-                flight["c"].wait_recv()
-                out[core, y, rng] = a2[rng] + r4[rng]
-                if inner_level > 0:
-                    flight["b"].start()
-                for copy in flight["y2"]:
-                    copy.start()
-        elif 0 < back < middle:
-
-            @pl.when(level == inner_level - back)
-            def _():
-                flight["b"].wait_recv()
-                if back < inner_level:
-                    flight["b"].start()
-                for copy in flight["y2"]:
-                    copy.start()
-
-        if back == middle:
-            for copy in flight["y2"]:
-                copy.wait_recv()
-            flight["core2"].start()
-        elif back == middle + 1:
-            flight["core2"].wait_recv()
-
-    for flight in flights:
-        flight["core"].start()
-    for flight, (low, high) in zip(flights, bounds):
-        rng = pl.ds(low, high - low)
-        flight["core"].wait_recv()
-        r1[:, rng] = r1[:, rng] + part[core, :, rng]
-        for copy in flight["y"]:
-            copy.start()
-    stages = 2 * middle + 2
-    for t in range(len(bounds) + stages - 1):
-        for stage in reversed(range(stages)):
-            if 0 <= t - stage < len(bounds):
-                step(stage, t - stage)
-    for flight in flights:
-        for copy in [flight["core"], flight["core2"]] + flight["y"] + flight["y2"]:
-            copy.wait_send()
-
-        @pl.when(level < inner_level)
-        def _():
-            flight["z"].wait_send()
-
-        @pl.when(level == inner_level)
-        def _():
-            flight["c"].wait_send()
-
-        @pl.when(level > 0)
-        def _():
-            flight["b"].wait_send()
 
 
 def local(
@@ -418,12 +460,15 @@
     smem = pl.BlockSpec(memory_space=pltpu.SMEM)
     sem = pltpu.SemaphoreType.DMA
     hbm = pl.BlockSpec(memory_space=pltpu.HBM)
-    used = orbitals // LANES * 2 * width + width + 8
-    height = -(-used // (count * 8)) * 8
+    pairs = count // 2
+    piece, tail = 2 * width // count, width // count
+    height = orbitals // LANES * piece + tail + 8
+    chunks = len(chunk_bounds(piece, tail + 8, orbitals // LANES))
+    one, many = sem((chunks,)), sem((chunks, pairs - 1))
     depth = rows // BLOCK * NEAR * SLOT
-    part = pl.pallas_call(
-        lambda *refs: compute_kernel(count, *refs),
-        out_shape=jax.ShapeDtypeStruct((count * height, LANES), F32),
+    reduced = pl.pallas_call(
+        lambda *refs: step_kernel(count, walks, *refs),
+        out_shape=jax.ShapeDtypeStruct((2, pairs, height, LANES), F32),
         in_specs=[smem] * 3 + [hbm] * 11,
         out_specs=vmem,
         scratch_shapes=[
@@ -450,11 +495,22 @@
             VM((row_local, width), BF16),
             VM((3 * rows, 2 * rows), F32),
             VM((walkers, width, rows), F32),
-        ],
+            VM((2, pairs, height, LANES), F32),
+            VM((pairs, height, LANES), F32),
+            VM((pairs - 1, height, LANES), F32),
+            VM((height, LANES), F32),
+            VM((height, LANES), F32),
+            VM((height, LANES), F32),
+        ]
+        + [one] * 2
+        + [many] * 2
+        + [one] * 6
+        + [many] * 2
+        + [one] * 2,
         compiler_params=pltpu.CompilerParams(
-            collective_id=0, has_side_effects=True, vmem_limit_bytes=40 * 1024 * 1024
+            collective_id=0, has_side_effects=True, vmem_limit_bytes=VMEM_MIB * 1024 * 1024
         ),
-        name="local_step",
+        name="whole_step",
     )(
         near_atoms.T,
         pair_list.T,
@@ -471,41 +527,16 @@
         w_orb.reshape(2 * width, orbitals),
         target.reshape(row_local, orbitals),
     )
-    pairs = count // 2
-    chunks = len(chunk_bounds(height))
-    one, many = sem((chunks,)), sem((chunks, pairs - 1))
-    reduced = pl.pallas_call(
-        lambda *refs: reduce_kernel(pairs, walks, *refs),
-        out_shape=jax.ShapeDtypeStruct((2, pairs, height, LANES), F32),
-        in_specs=[vmem],
-        out_specs=vmem,
-        scratch_shapes=[
-            VM((pairs, height, LANES), F32),
-            VM((pairs - 1, height, LANES), F32),
-            VM((height, LANES), F32),
-            VM((height, LANES), F32),
-            VM((height, LANES), F32),
-        ]
-        + [one] * 2
-        + [many] * 2
-        + [one] * 6
-        + [many] * 2
-        + [one] * 2,
-        compiler_params=pltpu.CompilerParams(
-            collective_id=1, has_side_effects=True, vmem_limit_bytes=40 * 1024 * 1024
-        ),
-        name="sum_all",
-    )(part.reshape(2, pairs, height, LANES))
-    flat = reduced.reshape(count * height, LANES)
-    base = orbitals // LANES * 2 * width
+    pieces = reduced.reshape(count, height, LANES)
+    base = orbitals // LANES * piece
     grad_orb = (
-        flat[:base]
-        .reshape(orbitals // LANES, 2, width, LANES)
-        .transpose(1, 2, 0, 3)
+        pieces[:, :base]
+        .reshape(count, orbitals // LANES, piece, LANES)
+        .transpose(0, 2, 1, 3)
         .reshape(2, width, orbitals)
     )
-    grad_out = flat[base : base + width]
-    loss = flat[base + width, :1]
+    grad_out = pieces[:, base : base + tail].reshape(width, width)
+    loss = pieces[0, base + tail, :1]
     return (grad_orb, grad_out, loss)
 
 

time: 88.2 us -> 70.7 us (0.80)
  Pallas kernels: 72.6 us -> 61.7 us
  local copies, waits for them, and re-layouts: 14.5 us -> 8.03 us
    unnamed x28 -> x0, local copies, waits for them, and re-layouts: 11.5 us -> none
    pallas_call x2 -> x1, Pallas kernels: 72.6 us -> 61.7 us  [local(): pl.pallas_call(lambda *refs: step_kernel(count, walks, *refs), out_shape=...]
    slice x3, local copies, waits for them, and re-layouts: 1.37 us -> 4.6 us  [the longest x1 1.73 us: local(): pieces[:, :base].reshape(count, orbitals // LANES, piece, LANES)]
    reshape x1 -> x2, local copies, waits for them, and re-layouts: 1.58 us -> 3.43 us  [local(): grad_orb = pieces[:, :base].reshape(count, orbitals // LANES, piece, LANE...]
where the time goes in v3:
time: 70.7 us; the launch traced here: 70.4 us
  Pallas kernels  61.7 us (87%)
  local copies, waits for them, and re-layouts  8.03 us (11%)
    pallas_call x1, Pallas kernels, local(): pl.pallas_call(lambda *refs: step_kernel(count, walks, *refs), out_shape=...  61.7 us
    reshape x2, local copies, waits for them, and re-layouts, local(): grad_orb = pieces[:, :base].reshape(count, orbitals // LANES, piece, LANE...  3.43 us
    slice x1, local copies, waits for them, and re-layouts, local(): pieces[:, :base].reshape(count, orbitals // LANES, piece, LANES)  1.73 us
    slice x1, local copies, waits for them, and re-layouts, local(): grad_out = pieces[:, base:base + tail].reshape(width, width)  1.67 us

profile of v3, /device:TPU:0, one launch (start us, length us, event | category | flops | bytes accessed | tf_op | source)
XLA Modules:
  0.0 70.4 jit_solution(12799999649055971425)
XLA Ops:
  0.6 61.7 %whole_step.1 = f32[2,2,584,256]{3,2,1,0:T(8,128)} custom-call(s32[2,8]{1,0:T(2,128)} %bitcast.24, s32[4,8]{1,0:T(4,128)} %bitcast.22, s32[1,8]{1,0:T(1,128)} %bitcast.25, f32[25,256]{1,0:T(8,128)} %refs_3_.1, f32[3,25]{1,0:T(4,128)} %bitcast.23, f32[3,4,128]{2,1,0:T(4,128)} %refs_5_.1, s32[1,128]{1,0:T(1,128)} %bitcast.26, f32[2,256]{1,0:T(2,128)} %refs_7_.1, ...), custom_call_target="tpu_custom_call" | custom-call | tf_op jit(solution)/shard_map/whole_step/pallas_call | solution.py:469
  62.4 1.2 %slice.14 = f32[1,1,1]{2,1,0:T(1,128)} slice(f32[4,584,256]{2,1,0:T(8,128)} %bitcast.14), slice={[0:1], [576:577], [0:1]} | slice | bytes 8 | tf_op jit(solution)/shard_map/slice | solution.py:539
  63.6 1.7 %slice.13 = f32[4,64,256]{2,1,0:T(8,128)} slice(f32[4,584,256]{2,1,0:T(8,128)} %bitcast.15), slice={[0:4], [512:576], [0:256]} | slice | bytes 524288 | tf_op jit(solution)/shard_map/slice | solution.py:538
  65.3 1.7 %slice.12 = f32[4,512,256]{2,1,0:T(8,128)S(1)} slice(f32[4,584,256]{2,1,0:T(8,128)} %bitcast.16), slice={[0:4], [0:512], [0:256]} | slice | bytes 4194304 | tf_op jit(solution)/shard_map/slice | solution.py:533
  67.0 1.4 %copy.19 = f32[4,4,128,256]{3,1,2,0:T(4,128)S(1)} copy(f32[4,4,128,256]{3,2,1,0:T(8,128)S(1)} %bitcast.17) | data formatting | bytes 4194304 | tf_op jit(solution)/shard_map/reshape | solution.py:534
  68.3 2.1 %reshape.36 = f32[2,256,1024]{2,1,0:T(8,128)} reshape(f32[4,128,4,256]{3,2,1,0:T(4,128)S(1)} %bitcast.18) | data formatting | bytes 4194304 | tf_op jit(solution)/shard_map/reshape | solution.py:536

commit v4 on v3

--- a/solution.py
+++ b/solution.py
@@ -14,7 +14,7 @@
 KMAX = 4
 SLOT = 32
 LANES = 256
-LAG = 2
+LAG = 3
 VMEM_MIB = 62
 F32 = jnp.float32
 BF16 = jnp.bfloat16
@@ -28,7 +28,12 @@
     return edges + [(piece * columns, piece * columns + extra)]
 
 
-def make_steps(pairs, walks, bounds, part, out, r1, r2, a2, r3, r4, *sems):
+def make_steps(pairs, walks, bounds, piece, tail, results, part, out, r1, r2, a2, r3, r4, *sems):
+    g_orb, g_out, g_loss = results
+    final_sem = sems[-1]
+    sems = sems[:-1]
+    columns = (len(bounds) - 1) // 2
+    finals = []
     send_core, recv_core, send_y, recv_y, send_z, recv_z, send_c, recv_c, send_b, recv_b = sems[:10]
     send_y2, recv_y2, send_core2, recv_core2 = sems[10:]
     elec = lax.axis_index("elec")
@@ -142,8 +147,30 @@
             for copy in flight["y2"]:
                 copy.wait_recv()
             flight["core2"].start()
+            write(c, core)
         elif back == middle + 1:
             flight["core2"].wait_recv()
+            write(c, 1 - core)
+
+    def emit(src, dst):
+        copy = pltpu.make_async_copy(src, dst, final_sem.at[len(finals)])
+        copy.start()
+        finals.append(copy)
+
+    def write(c, side):
+        low, high = bounds[c]
+        for v in range(pairs):
+            q = side * pairs + v
+            if c < 2 * columns:
+                col = c // 2
+                start = pl.multiple_of(q * piece + low - col * piece, 8)
+                emit(
+                    out.at[side, v, low:high],
+                    g_orb.at[pl.ds(start, high - low), col * LANES : (col + 1) * LANES],
+                )
+            else:
+                start = pl.multiple_of(q * tail, 8)
+                emit(out.at[side, v, low : low + tail], g_out.at[pl.ds(start, tail)])
 
     def begin(c):
         flights[c]["core"].start()
@@ -169,6 +196,10 @@
     total_steps = len(bounds) + LAG * stages
 
     def drain():
+        low = bounds[-1][0]
+        emit(out.at[0, 0, low + tail : low + tail + 8, :128], g_loss)
+        for copy in finals:
+            copy.wait()
         for flight in flights:
             for copy in [flight["core"], flight["core2"]] + flight["y"] + flight["y2"]:
                 copy.wait_send()
@@ -200,13 +231,12 @@
     spin,
     *rest,
 ):
-    outer, inner = rest[:7], rest[8:]
-    out = rest[7]
+    outer, results, inner = rest[:7], rest[7:10], rest[10:]
     gemb, gpos, gep, gsp = inner[:4]
     held = inner[4:11]
     spin_emb, w_query, w_key, w_value, w_out, w_orb, target = held
     send, recv, local_sem = inner[11:14]
-    pstack, estack, e_s, q_s, k_s, vt_s, h_s, bias_s, att_s, part = inner[14:24]
+    pstack, estack, e_s, q_s, k_s, vt_s, h_s, bias_s, att_s, part, out = inner[14:25]
     me = lax.axis_index("elec")
     barrier = pltpu.get_barrier_semaphore()
     for k in range(count - 1):
@@ -394,7 +424,7 @@
     columns_total = orbitals // LANES
     bounds = chunk_bounds(piece, tail + 8, columns_total)
     begin, advance, drain, total_steps = make_steps(
-        pairs, walks, bounds, part, out, *inner[24:]
+        pairs, walks, bounds, piece, tail, results, part, out, *inner[25:]
     )
     moved = 0
     share = 1.0 / (walkers * rows * count * lax.axis_size("walk"))
@@ -456,7 +486,6 @@
     count, walks = lax.axis_size("elec"), lax.axis_size("walk")
     width, orbitals = w_query.shape[0], w_orb.shape[2]
     row_local = walkers * rows
-    vmem = pl.BlockSpec(memory_space=VM)
     smem = pl.BlockSpec(memory_space=pltpu.SMEM)
     sem = pltpu.SemaphoreType.DMA
     hbm = pl.BlockSpec(memory_space=pltpu.HBM)
@@ -466,11 +495,16 @@
     chunks = len(chunk_bounds(piece, tail + 8, orbitals // LANES))
     one, many = sem((chunks,)), sem((chunks, pairs - 1))
     depth = rows // BLOCK * NEAR * SLOT
-    reduced = pl.pallas_call(
+    finals = pairs * 2 * chunks + 1
+    grad_orb, grad_out, loss = pl.pallas_call(
         lambda *refs: step_kernel(count, walks, *refs),
-        out_shape=jax.ShapeDtypeStruct((2, pairs, height, LANES), F32),
+        out_shape=(
+            jax.ShapeDtypeStruct((2 * width, orbitals), F32),
+            jax.ShapeDtypeStruct((width, width), F32),
+            jax.ShapeDtypeStruct((8, 128), F32),
+        ),
         in_specs=[smem] * 3 + [hbm] * 11,
-        out_specs=vmem,
+        out_specs=(hbm,) * 3,
         scratch_shapes=[
             VM((count, ATOM_DEV, width), F32),
             VM((count, 3, ATOM_DEV), F32),
@@ -496,6 +530,7 @@
             VM((3 * rows, 2 * rows), F32),
             VM((walkers, width, rows), F32),
             VM((2, pairs, height, LANES), F32),
+            VM((2, pairs, height, LANES), F32),
             VM((pairs, height, LANES), F32),
             VM((pairs - 1, height, LANES), F32),
             VM((height, LANES), F32),
@@ -506,7 +541,8 @@
         + [many] * 2
         + [one] * 6
         + [many] * 2
-        + [one] * 2,
+        + [one] * 2
+        + [sem((finals,))],
         compiler_params=pltpu.CompilerParams(
             collective_id=0, has_side_effects=True, vmem_limit_bytes=VMEM_MIB * 1024 * 1024
         ),
@@ -527,17 +563,7 @@
         w_orb.reshape(2 * width, orbitals),
         target.reshape(row_local, orbitals),
     )
-    pieces = reduced.reshape(count, height, LANES)
-    base = orbitals // LANES * piece
-    grad_orb = (
-        pieces[:, :base]
-        .reshape(count, orbitals // LANES, piece, LANES)
-        .transpose(0, 2, 1, 3)
-        .reshape(2, width, orbitals)
-    )
-    grad_out = pieces[:, base : base + tail].reshape(width, width)
-    loss = pieces[0, base + tail, :1]
-    return (grad_orb, grad_out, loss)
+    return (grad_orb.reshape(2, width, orbitals), grad_out, loss[0, :1])
 
 
 def solution(mesh):

time: 70.7 us -> 62.6 us (0.89)
  Pallas kernels: 61.7 us -> 56 us
  local copies, waits for them, and re-layouts: 8.03 us -> 5.1 us
    pallas_call x1, Pallas kernels: 61.7 us -> 56 us  [local(): pl.pallas_call(lambda *refs: step_kernel(count, walks, *refs), out_shape=...]
    unnamed x0 -> x4, local copies, waits for them, and re-layouts: none -> 3.91 us
    reshape x2 -> x0, local copies, waits for them, and re-layouts: 3.43 us -> none  [local(): grad_orb = pieces[:, :base].reshape(count, orbitals // LANES, piece, LANE...]
    slice x3 -> x1, local copies, waits for them, and re-layouts: 4.6 us -> 1.19 us  [local(): return (grad_orb.reshape(2, width, orbitals), grad_out, loss[0, :1])]
where the time goes in v4:
time: 62.6 us; the launch traced here: 61.7 us
  Pallas kernels  56 us (89%)
  local copies, waits for them, and re-layouts  5.1 us (8%)
  between operations  0.65 us (1%)
    pallas_call x1, Pallas kernels, local(): pl.pallas_call(lambda *refs: step_kernel(count, walks, *refs), out_shape=...  56 us
    unnamed x4, local copies, waits for them, and re-layouts  3.91 us

profile of v4, /device:TPU:0, one launch (start us, length us, event | category | flops | bytes accessed | tf_op | source)
XLA Modules:
  0.0 61.7 jit_solution(4174793395141262059)
XLA Ops:
  0.6 56.0 %whole_step.1 = (f32[512,1024]{1,0:T(8,128)}, f32[256,256]{1,0:T(8,128)}, f32[8,128]{1,0:T(8,128)}) custom-call(s32[2,8]{1,0:T(2,128)} %bitcast.14, s32[4,8]{1,0:T(4,128)} %bitcast.12, s32[1,8]{1,0:T(1,128)} %bitcast.15, f32[25,256]{1,0:T(8,128)} %refs_3_.1, f32[3,25]{1,0:T(4,128)} %bitcast.13, f32[3,4,128]{2,1,0:T(4,128)} %refs_5_.1, s32[1,128]{1,0:T(1,128)} %bitcast.16, ...), custom_call_target="tpu_custom_call" | custom-call | tf_op jit(solution)/shard_map/whole_step/pallas_call | solution.py:499
  56.6 1.2 %slice.3 = f32[1,1]{1,0:T(1,128)} slice(f32[8,128]{1,0:T(8,128)} %get-tuple-element.8), slice={[0:1], [0:1]} | slice | bytes 8 | tf_op jit(solution)/shard_map/slice | solution.py:566
  57.8 0.0 copy-start
  57.8 3.2 %copy.19 = f32[2,256,1024]{2,1,0:T(8,128)} copy(f32[2,256,1024]{2,1,0:T(8,128)} %bitcast.9) | data formatting | bytes 4194304
  61.0 0.0 copy-done
  61.0 0.7 %copy.20 = f32[256,256]{1,0:T(8,128)} copy(f32[256,256]{1,0:T(8,128)S(1)} %copy-done) | data formatting | bytes 524288
Async XLA Ops:
  57.8 3.2 %copy-start = (f32[256,256]{1,0:T(8,128)S(1)}, f32[256,256]{1,0:T(8,128)}, u32[]{:S(2)}) copy-start(f32[256,256]{1,0:T(8,128)} %get-tuple-element.13) | copy-start | bytes 786436
